TPU v7x, 256 devices: a whole 4x4x8 slice. The times are simulated.
256 devices in a mesh: pair: 32 (over y, x, core), occ: 8 (over z).
Axes of the slice: x: 4, y: 4, z: 8, core: 2. Of those that a mesh axis runs over, the one named last changes fastest.
Arguments:
- half_ints: bfloat16 [8, 12288, 6144], P('occ', 'pair'), may hold values from -6 to 6
- pair_coef: bfloat16 [512, 12288], P('occ'), may hold values from -0.078125 to 0.078125
- mo_virtual: bfloat16 [5632, 6144], P('pair'), may hold values from -0.078125 to 0.078125
- screen: int32 [192], replicated, may hold values 0 or 1
- slot_block: int32 [192], replicated, may hold values from 0 to 191, each once
Outputs:
- mo_block: bfloat16 [5632, 8, 512], P('pair', 'occ')
Inputs may be any that keep to these rules, and one draw needn't show every extreme that they name: `screen`: 1 where the pair block survives screening, 0 where it is dropped. `slot_block`: each logical pair block stands in exactly one storage slot; index k of pair holds slots k * 6 to k * 6 + 5.
All inputs are finite; a program needn't handle non-finite values.
Results may differ from a plain program's by a relative error of at most 0.0049.
Values may be sent and summed in bfloat16 or wider, within the bound.
No kernel may reach another device: no remote copies, remote signals or barrier semaphores. Data moves between devices by JAX's collectives and lax.ppermute only.
A program may use at most 128 MiB of HBM per device.

v0:
```python
import jax
import jax.numpy as jnp
from jax import lax
from jax.sharding import PartitionSpec as P


def shards(half_ints, pair_coef, mo_virtual, screen, slot_block):
    coef_all = lax.all_gather(pair_coef, "occ", axis=0, tiled=True)
    occ_width = coef_all.shape[0]
    block_count = screen.shape[0]
    block_width = coef_all.shape[1] // block_count
    masked_coef = (
        coef_all.reshape(occ_width, block_count, block_width)
        * screen.astype(jnp.bfloat16)[None, :, None]
    )
    selected = jnp.take(masked_coef, slot_block, axis=1).reshape(
        occ_width, block_count * block_width
    )
    local_pairs = half_ints.shape[1]
    own_index = lax.axis_index("pair")
    local_cols = lax.dynamic_slice_in_dim(selected, own_index * local_pairs, local_pairs, 1)
    summed_pairs = lax.psum_scatter(
        jnp.einsum("jq,iqn->nij", local_cols, half_ints, preferred_element_type=jnp.float32),
        "pair",
        scatter_dimension=0,
        tiled=True,
    )
    occ_pair = summed_pairs.astype(jnp.bfloat16)
    item_width = occ_pair.shape[1] * occ_pair.shape[2]
    virt_count = mo_virtual.shape[0]
    block_part = lax.all_gather(occ_pair, "pair", axis=0, tiled=True)
    flat_rows = block_part.reshape(block_part.shape[0], item_width)
    folded = jnp.dot(mo_virtual, flat_rows, preferred_element_type=jnp.float32)
    return folded.reshape(virt_count, occ_pair.shape[1], occ_pair.shape[2]).astype(jnp.bfloat16)


def solution(mesh):
    placed = (P("occ", "pair", None), P("occ", None), P("pair", None), P(), P())
    return jax.shard_map(
        shards, mesh=mesh, in_specs=placed, out_specs=P("pair", "occ", None), check_vma=False
    )
```

profile of v0, /device:TPU:1, one launch (start us, length us, event | category | flops | bytes accessed | tf_op | source)
XLA Modules:
  0.0 1388.3 jit_solution(8234210186869820136)
XLA Ops:
  6.5 0.0 copy-start
  6.5 0.0 all-gather.3.cloned.1.call-start
  6.5 0.7 all-gather.3.cloned.1.call-update
  7.3 0.0 all-gather.5.cloned.1.call-start
  7.3 0.7 convert_element_type.15
  8.0 0.7 compare_and_fusion
  8.7 0.1 broadcast_in_dim.17
  8.8 0.1 broadcast_in_dim.18
  8.9 0.1 dynamic-slice.2
  9.0 1.3 dynamic-slice
  10.9 0.7 compare_select_fusion
  11.6 134.8 %all-gather.3.cloned.1.call-done = bf16[512,12288]{1,0:T(8,128)(2,1)} async-done(((bf16[64,12288]{1,0:T(8,128)(2,1)}), bf16[512,12288]{1,0:T(8,128)(2,1)}) %all-gather.3.cloned.1.call-update) | async-done | bytes 12582928 | tf_op jit(solution)/shard_map/all_gather | solution.py:8
  146.4 16.6 %copy.7 = bf16[512,12288]{0,1:T(8,128)(2,1)} copy(bf16[512,12288]{1,0:T(8,128)(2,1)} %all-gather.3.cloned.1.call-done) | data formatting | bytes 25165824 | tf_op jit(solution)/shard_map/all_gather | solution.py:8
  163.0 10.6 broadcast_multiply_fusion
  173.6 12.8 gather_fusion
  186.5 10.5 convolution_bitcast_fusion
  196.9 27.0 %copy.8 = f32[6144,1,512]{2,1,0:T(1,128)} copy(f32[6144,1,512]{0,2,1:T(8,128)} %convolution_bitcast_fusion) | data formatting | bytes 25165824 | tf_op jit(solution)/shard_map/jq,iqn->nij/transpose | solution.py:23
  224.0 1093.3 %all-reduce.2 = bf16[6144,1,512]{2,1,0:T(2,128)(2,1)} all-reduce(f32[6144,1,512]{2,1,0:T(1,128)} %copy.8), channel_id=2, replica_groups=mesh['pair'=32,'occ'=8] {'pair'}, use_global_device_ids=true, to_apply=%region_0.1.clone | all-reduce | flops 3145728 | bytes 18874368
  1317.3 1.4 dynamic-slice_convert_fusion
  1318.7 0.7 copy.9
  1319.4 0.0 all-gather.5.cloned.1.call-update
  1319.4 57.3 %all-gather.5.cloned.1.call-done = bf16[6144,1,512]{2,0,1:T(8,128)(2,1)} async-done(((bf16[192,1,512]{2,0,1:T(8,128)(2,1)}), bf16[6144,1,512]{2,0,1:T(8,128)(2,1)}) %all-gather.5.cloned.1.call-update) | async-done | bytes 6291472 | tf_op jit(solution)/shard_map/all_gather | solution.py:31
  1376.7 0.0 copy-done
  1376.7 4.7 fusion.6
  (1 shorter events, 0.0 us)
Async XLA Ops:
  6.5 1370.2 %copy-start = (bf16[176,6144]{1,0:T(8,128)(2,1)S(1)}, bf16[176,6144]{1,0:T(8,128)(2,1)}, u32[]{:S(2)}) copy-start(bf16[176,6144]{1,0:T(8,128)(2,1)} %param.7) | copy-start | bytes 6488068
  6.5 139.9 %all-gather.3.cloned.1.call-start = ((), (), s32[]{:S(2)}) async-start(), calls=%async_computation | async-start | bytes 14155776 | tf_op jit(solution)/shard_map/all_gather | solution.py:8
  7.3 1369.5 %all-gather.5.cloned.1.call-start = ((), (), s32[]{:S(2)}) async-start(), calls=%async_computation.1 | async-start | bytes 6488064 | tf_op jit(solution)/shard_map/all_gather | solution.py:31
Sparse Core Ops, SparseCore 0:
  9.1 137.2 all-gather.2
  1319.6 57.1 all-gather.4
where the time goes:
time: 1390 us
  blocking collectives  1090 us (78%)
  waiting for transfers between devices  193 us (14%)
  local copies, waits for them, and re-layouts  60.1 us (4%)
  matrix products  15.2 us (1%)
  between operations  14.1 us (1%)
    unnamed x1, blocking collectives  1090 us
    all_gather x1, waiting for transfers between devices, shards(): coef_all = lax.all_gather(pair_coef, 'occ', axis=0, tiled=True)  135 us
    all_gather x1, waiting for transfers between devices, shards(): block_part = lax.all_gather(occ_pair, 'pair', axis=0, tiled=True)  57.3 us
  transfers between devices with their start and end apart: 2, of which 2 were waited for; matrix products, arithmetic and copies ran while one was open for 0% of the time, Pallas kernels for 0%

commit v1 on v0

v1 whole, which is shorter than its diff:
```python
import jax
import jax.numpy as jnp
from jax import lax
from jax.sharding import Mesh
from jax.sharding import PartitionSpec as P

Y, X, C, Z = 4, 4, 2, 8
SIZE = {"y": Y, "x": X, "core": C, "z": Z}


def shift(value, axis, step):
    size = SIZE[axis]
    return lax.ppermute(value, axis, [(i, (i + step) % size) for i in range(size)])


def rows(value, block, height):
    return lax.dynamic_slice_in_dim(value, block * height, height, 0)


def reduce_scatter(part, axis):
    size = SIZE[axis]
    height = part.shape[0] // size
    me = lax.axis_index(axis)
    got = []
    for step in range(1, size):
        out = rows(part, (me + step) % size, height).astype(jnp.bfloat16)
        got.append(shift(out, axis, step))
    total = rows(part, me, height)
    for piece in got:
        total = total + piece.astype(jnp.float32)
    return total


def gather(own, axis):
    size = SIZE[axis]
    height = own.shape[0]
    me = lax.axis_index(axis)
    whole = jnp.zeros((height * size, own.shape[1]), own.dtype)
    whole = lax.dynamic_update_slice_in_dim(whole, own, me * height, 0)
    for step in range(1, size):
        piece = shift(own, axis, step)
        whole = lax.dynamic_update_slice_in_dim(whole, piece, ((me - step) % size) * height, 0)
    return whole


def shards(half_ints, pair_coef, mo_virtual, screen, slot_block):
    core = lax.axis_index("core")
    own = (lax.axis_index("y") * X + lax.axis_index("x")) * C + core
    ints = half_ints[0]
    pairs, basis = ints.shape
    count = screen.shape[0]
    width = pair_coef.shape[1] // count
    held = pairs // width
    half = basis // 2

    blocks = lax.dynamic_slice_in_dim(slot_block, own * held, held, 0)
    picked = [
        lax.dynamic_slice_in_dim(pair_coef, blocks[s] * width, width, 1) * screen[blocks[s]].astype(jnp.bfloat16)
        for s in range(held)
    ]
    chosen = jnp.concatenate(picked, axis=1)
    mine = lax.all_gather(chosen, "z", axis=0, tiled=True)
    theirs = shift(mine, "core", 1)

    kept = lax.dynamic_slice_in_dim(ints, core * half, half, 1)
    given = lax.dynamic_slice_in_dim(ints, (1 - core) * half, half, 1)
    taken = shift(given, "core", 1)
    virt_kept = lax.dynamic_slice_in_dim(mo_virtual, core * half, half, 1)
    virt_given = lax.dynamic_slice_in_dim(mo_virtual, (1 - core) * half, half, 1)
    virt_taken = shift(virt_given, "core", 1)

    over = (((0,), (1,)), ((), ()))
    part = lax.dot_general(kept, mine, over, preferred_element_type=jnp.float32) + lax.dot_general(
        taken, theirs, over, preferred_element_type=jnp.float32
    )
    first, second = part[: half // 2], part[half // 2 :]
    first = reduce_scatter(reduce_scatter(first, "x"), "y").astype(jnp.bfloat16)
    second = reduce_scatter(reduce_scatter(second, "y"), "x").astype(jnp.bfloat16)
    first = gather(gather(first, "y"), "x")
    second = gather(gather(second, "x"), "y")

    quarter = half // 2
    def fold(virt):
        return jnp.dot(virt[:, :quarter], first, preferred_element_type=jnp.float32) + jnp.dot(
            virt[:, quarter:], second, preferred_element_type=jnp.float32
        )

    passed = shift(fold(virt_taken), "core", 1)
    out = (fold(virt_kept) + passed).astype(jnp.bfloat16)
    return out[:, None, :]


def solution(mesh):
    split = Mesh(mesh.devices.reshape(Y, X, C, Z), ("y", "x", "core", "z"))
    pair = ("y", "x", "core")
    placed = (P("z", pair, None), P("z", None), P(pair, None), P(), P())
    return jax.shard_map(
        shards, mesh=split, in_specs=placed, out_specs=P(pair, "z", None), check_vma=False
    )
```

time: 1390 us -> 151 us (0.11)
  blocking collectives: 1090 us -> 20.6 us
  waiting for transfers between devices: 193 us -> 34.3 us
  starting transfers between devices: 0.04 us -> 48.2 us
  local copies, waits for them, and re-layouts: 60.1 us -> 12.6 us
    unnamed x1 -> x0, blocking collectives: 1090 us -> none
    all_gather x2 -> x0, waiting for transfers between devices: 192 us -> none  [the longest x1 135 us: shards(): coef_all = lax.all_gather(pair_coef, 'occ', axis=0, tiled=True)]
    ppermute x0 -> x28, starting transfers between devices: none -> 48.2 us  [shift(): lax.ppermute(value, axis, [(i, (i + step) % size) for i in range(size)])]
    ppermute x0 -> x28, waiting for transfers between devices: none -> 34.3 us  [shift(): lax.ppermute(value, axis, [(i, (i + step) % size) for i in range(size)])]
    transpose x1 -> x0, local copies, waits for them, and re-layouts: 27 us -> none  [shards(): jnp.einsum('jq,iqn->nij', local_cols, half_ints, preferred_element_type=j...]
    all_gather x0 -> x1, blocking collectives: none -> 20.6 us  [shards(): mine = lax.all_gather(chosen, 'z', axis=0, tiled=True)]
    all_gather x1 -> x0, local copies, waits for them, and re-layouts: 16.6 us -> none  [shards(): coef_all = lax.all_gather(pair_coef, 'occ', axis=0, tiled=True)]
  transfers between devices with their start and end apart: 2 -> 28, of which waited for: 2 -> 11; matrix products, arithmetic and copies ran while one was open for 0% -> 10% of each run, Pallas kernels for 0% -> 0%
where the time goes in v1:
time: 151 us
  starting transfers between devices  48.2 us (32%)
  waiting for transfers between devices  34.3 us (23%)
  blocking collectives  20.6 us (14%)
  between operations  19.2 us (13%)
  local copies, waits for them, and re-layouts  12.6 us (8%)
  matrix products  11.9 us (8%)
  other arithmetic  4.1 us (3%)
    ppermute x28, starting transfers between devices, shift(): lax.ppermute(value, axis, [(i, (i + step) % size) for i in range(size)])  48.2 us
    ppermute x28, waiting for transfers between devices, shift(): lax.ppermute(value, axis, [(i, (i + step) % size) for i in range(size)])  34.3 us
    all_gather x1, blocking collectives, shards(): mine = lax.all_gather(chosen, 'z', axis=0, tiled=True)  20.6 us
    dot_general x1, matrix products, shards(): lax.dot_general(taken, theirs, over, preferred_element_type=jnp.float32)  3.6 us
    dot_general x1, matrix products, shards(): lax.dot_general(kept, mine, over, preferred_element_type=jnp.float32)  3.51 us
    dynamic_slice x1, local copies, waits for them, and re-layouts, shards(): given = lax.dynamic_slice_in_dim(ints, (1 - core) * half, half, 1)  3.4 us
    add x2, other arithmetic, reduce_scatter(): total = total + piece.astype(jnp.float32)  3.07 us
  transfers between devices with their start and end apart: 28, of which 11 were waited for; matrix products, arithmetic and copies ran while one was open for 10% of the time, Pallas kernels for 0%

profile of v1, /device:TPU:1, one launch (start us, length us, event | category | flops | bytes accessed | tf_op | source)
XLA Modules:
  0.0 150.9 jit_solution(16672259934537298658)
XLA Ops:
  0.0 3.4 %dynamic-slice_bitcast_fusion = bf16[384,3072]{1,0:T(8,128)(2,1)} fusion(bf16[1,384,6144]{2,1,0:T(8,128)(2,1)} %param.5, s32[]{:T(128)S(6)} %select_n.224), kind=kLoop, calls=%fused_computation.3 | loop fusion | bytes 4718596 | tf_op jit(solution)/shard_map/dynamic_slice | solution.py:66
  3.4 3.2 %collective-permute-start = (bf16[384,3072]{1,0:T(8,128)(2,1)}, bf16[384,3072]{1,0:T(8,128)(2,1)}, u32[]{:S(2)}, u32[]{:S(2)}) collective-permute-start(bf16[384,3072]{1,0:T(8,128)(2,1)} %dynamic-slice_bitcast_fusion), channel_id=1, source_target_pairs={{0,8},{8,0},{1,9},{9,1},{2,10},{10,2},{3,11},{11,3},{4,12},{12,4},... | collective-permute-start | bytes 7077896 | tf_op jit(solution)/shard_map/ppermute | solution.py:13
  28.0 20.6 %all_gather.3 = bf16[512,384]{1,0:T(8,128)(2,1)S(1)} all-gather(bf16[64,384]{1,0:T(8,128)(2,1)S(1)} %concatenate.3), channel_id=1, replica_groups=mesh['y'=4,'x'=4,'core'=2,'z'=8] {'z'}, dimensions={0}, use_global_device_ids=true | all-gather | bytes 442368 | tf_op jit(solution)/shard_map/all_gather | solution.py:62
  48.6 6.4 %collective-permute-start.1 = (bf16[512,384]{1,0:T(8,128)(2,1)S(1)}, bf16[512,384]{1,0:T(8,128)(2,1)S(1)}, u32[]{:S(2)}, u32[]{:S(2)}) collective-permute-start(bf16[512,384]{1,0:T(8,128)(2,1)S(1)} %all_gather.3), channel_id=1, source_target_pairs={{0,8},{8,0},{1,9},{9,1},{2,10},{10,2},{3,11},{11,3},{4,12},{12,4},... | collective-permute-start | bytes 1179656 | tf_op jit(solution)/shard_map/ppermute | solution.py:13
  55.0 3.5 %fusion = f32[3072,512]{1,0:T(8,128)S(1)} fusion(bf16[512,384]{1,0:T(8,128)(2,1)S(1)} %all_gather.3, bf16[1,384,6144]{2,1,0:T(8,128)(2,1)} %param.5, s32[]{:T(128)S(6)} %select_n.210), kind=kOutput, calls=%fused_computation.1 | convolution fusion | flops 1207959552 | bytes 9043972 | tf_op jit(solution)/shard_map/dot_general | solution.py:73
  58.6 3.6 %convolution_add_fusion = f32[3072,512]{1,0:T(8,128)S(1)} fusion(f32[3072,512]{1,0:T(8,128)S(1)} %fusion, bf16[384,3072]{1,0:T(8,128)(2,1)} %collective-permute-done, bf16[512,384]{1,0:T(8,128)(2,1)S(1)} %collective-permute-done.1), kind=kOutput, calls=%fused_computation | convolution fusion | flops 1209532416 | bytes 15335424 | tf_op jit(solution)/shard_map/dot_general | solution.py:73
  62.2 2.3 %fusion.15 = (f32[1536,512]{1,0:T(8,128)S(1)}, f32[1536,512]{1,0:T(8,128)}) fusion(f32[3072,512]{1,0:T(8,128)S(1)} %convolution_add_fusion), kind=kLoop, calls=%fused_computation.58 | loop fusion | bytes 12582912 | tf_op jit(solution)/shard_map/slice | solution.py:76
  65.7 1.2 collective-permute-start.2
  66.9 2.5 %collective-permute-start.3 = (bf16[384,512]{1,0:T(8,128)(2,1)}, bf16[384,512]{1,0:T(8,128)(2,1)}, u32[]{:S(2)}, u32[]{:S(2)}) collective-permute-start(bf16[384,512]{1,0:T(8,128)(2,1)} %get-tuple-element.13), channel_id=1, source_target_pairs={{0,32},{16,48},{32,0},{48,16},{1,33},{17,49},{33,1},{49,17},{2,34}... | collective-permute-start | bytes 1179656 | tf_op jit(solution)/shard_map/ppermute | solution.py:13
  72.4 1.8 %dynamic-slice_convert_fusion.2 = (bf16[384,512]{1,0:T(8,128)(2,1)S(1)}, bf16[384,512]{1,0:T(8,128)(2,1)S(1)}, bf16[384,512]{1,0:T(8,128)(2,1)S(1)}) fusion(f32[1536,512]{1,0:T(8,128)} %get-tuple-element.10, s32[]{:T(128)S(6)} %select_n.252, s32[]{:T(128)S(6)} %select_n.254, s32[]{:T(128)S(6)} %select_n.253), kind=kLoop, calls=%fused_computation.13 | loop fusion | bytes 2359308 | tf_op jit(solution)/shard_map/convert_element_type | solution.py:26
  74.2 1.4 collective-permute-start.14
  75.6 2.4 %collective-permute-done.2 = bf16[384,512]{1,0:T(8,128)(2,1)} collective-permute-done((bf16[384,512]{1,0:T(8,128)(2,1)}, bf16[384,512]{1,0:T(8,128)(2,1)}, u32[]{:S(2)}, u32[]{:S(2)}) %collective-permute-start.2) | collective-permute-done | bytes 393248 | tf_op jit(solution)/shard_map/ppermute | solution.py:13
  78.0 2.9 %collective-permute-start.15 = (bf16[384,512]{1,0:T(8,128)(2,1)S(1)}, bf16[384,512]{1,0:T(8,128)(2,1)S(1)}, u32[]{:S(2)}, u32[]{:S(2)}) collective-permute-start(bf16[384,512]{1,0:T(8,128)(2,1)S(1)} %get-tuple-element.16), channel_id=1, source_target_pairs={{0,128},{64,192},{128,0},{192,64},{1,129},{65,193},{129,1},{193,65... | collective-permute-start | bytes 1179656 | tf_op jit(solution)/shard_map/ppermute | solution.py:13
  80.9 6.5 %collective-permute-done.3 = bf16[384,512]{1,0:T(8,128)(2,1)} collective-permute-done((bf16[384,512]{1,0:T(8,128)(2,1)}, bf16[384,512]{1,0:T(8,128)(2,1)}, u32[]{:S(2)}, u32[]{:S(2)}) %collective-permute-start.3) | collective-permute-done | bytes 393248 | tf_op jit(solution)/shard_map/ppermute | solution.py:13
  87.4 2.7 %collective-permute-start.16 = (bf16[384,512]{1,0:T(8,128)(2,1)S(1)}, bf16[384,512]{1,0:T(8,128)(2,1)S(1)}, u32[]{:S(2)}, u32[]{:S(2)}) collective-permute-start(bf16[384,512]{1,0:T(8,128)(2,1)S(1)} %get-tuple-element.15), channel_id=1, source_target_pairs={{0,192},{64,0},{128,64},{192,128},{1,193},{65,1},{129,65},{193,129... | collective-permute-start | bytes 1179656 | tf_op jit(solution)/shard_map/ppermute | solution.py:13
  90.1 1.7 %convert_add_fusion.1 = f32[384,512]{1,0:T(8,128)S(1)} fusion(bf16[384,512]{1,0:T(8,128)(2,1)} %collective-permute-done.4, bf16[384,512]{1,0:T(8,128)(2,1)} %collective-permute-done.3, bf16[384,512]{1,0:T(8,128)(2,1)} %collective-permute-done.2, f32[1536,512]{1,0:T(8,128)} %copy-done.4, s32[]{:T(128)S(6)} %select_n.225), kind=kLoop, calls=%fused_computation.14 | loop fusion | flops 1179648 | bytes 2752516 | tf_op jit(solution)/shard_map/add | solution.py:30
  92.2 1.6 %collective-permute-start.6 = (bf16[96,512]{1,0:T(8,128)(2,1)S(1)}, bf16[96,512]{1,0:T(8,128)(2,1)S(1)}, u32[]{:S(2)}, u32[]{:S(2)}) collective-permute-start(bf16[96,512]{1,0:T(8,128)(2,1)S(1)} %get-tuple-element.25), channel_id=1, source_target_pairs={{0,128},{64,192},{128,0},{192,64},{1,129},{65,193},{129,1},{193,65... | collective-permute-start | bytes 294920 | tf_op jit(solution)/shard_map/ppermute | solution.py:13
  93.8 2.1 %collective-permute-done.15 = bf16[384,512]{1,0:T(8,128)(2,1)S(1)} collective-permute-done((bf16[384,512]{1,0:T(8,128)(2,1)S(1)}, bf16[384,512]{1,0:T(8,128)(2,1)S(1)}, u32[]{:S(2)}, u32[]{:S(2)}) %collective-permute-start.15) | collective-permute-done | bytes 393248 | tf_op jit(solution)/shard_map/ppermute | solution.py:13
  95.9 2.7 %collective-permute-done.16 = bf16[384,512]{1,0:T(8,128)(2,1)S(1)} collective-permute-done((bf16[384,512]{1,0:T(8,128)(2,1)S(1)}, bf16[384,512]{1,0:T(8,128)(2,1)S(1)}, u32[]{:S(2)}, u32[]{:S(2)}) %collective-permute-start.16) | collective-permute-done | bytes 393248 | tf_op jit(solution)/shard_map/ppermute | solution.py:13
  98.6 1.4 convert_add_fusion
  100.7 2.5 %collective-permute-start.18 = (bf16[96,512]{1,0:T(8,128)(2,1)S(1)}, bf16[96,512]{1,0:T(8,128)(2,1)S(1)}, u32[]{:S(2)}, u32[]{:S(2)}) collective-permute-start(bf16[96,512]{1,0:T(8,128)(2,1)S(1)} %get-tuple-element.28), channel_id=1, source_target_pairs={{0,32},{16,48},{32,0},{48,16},{1,33},{17,49},{33,1},{49,17},{2,34}... | collective-permute-start | bytes 294920 | tf_op jit(solution)/shard_map/ppermute | solution.py:13
  103.2 1.3 collective-permute-start.19
  104.5 1.7 %collective-permute-start.8 = (bf16[96,512]{1,0:T(8,128)(2,1)S(1)}, bf16[96,512]{1,0:T(8,128)(2,1)S(1)}, u32[]{:S(2)}, u32[]{:S(2)}) collective-permute-start(bf16[96,512]{1,0:T(8,128)(2,1)S(1)} %get-tuple-element.6), channel_id=1, source_target_pairs={{0,64},{64,128},{128,192},{192,0},{1,65},{65,129},{129,193},{193,1... | collective-permute-start | bytes 294920 | tf_op jit(solution)/shard_map/ppermute | solution.py:13
  106.2 3.1 %collective-permute-start.9 = (bf16[96,512]{1,0:T(8,128)(2,1)S(1)}, bf16[96,512]{1,0:T(8,128)(2,1)S(1)}, u32[]{:S(2)}, u32[]{:S(2)}) collective-permute-start(bf16[96,512]{1,0:T(8,128)(2,1)S(1)} %get-tuple-element.6), channel_id=1, source_target_pairs={{0,128},{64,192},{128,0},{192,64},{1,129},{65,193},{129,1},{193,65... | collective-permute-start | bytes 294920 | tf_op jit(solution)/shard_map/ppermute | solution.py:13
  110.8 1.3 collective-permute-start.21
  112.4 1.7 %collective-permute-start.22 = (bf16[96,512]{1,0:T(8,128)(2,1)S(1)}, bf16[96,512]{1,0:T(8,128)(2,1)S(1)}, u32[]{:S(2)}, u32[]{:S(2)}) collective-permute-start(bf16[96,512]{1,0:T(8,128)(2,1)S(1)} %get-tuple-element.8), channel_id=1, source_target_pairs={{0,48},{16,0},{32,16},{48,32},{1,49},{17,1},{33,17},{49,33},{2,50}... | collective-permute-start | bytes 294920 | tf_op jit(solution)/shard_map/ppermute | solution.py:13
  117.6 1.2 collective-permute-start.24
  119.1 10.2 %collective-permute-done.11 = bf16[384,512]{1,0:T(8,128)(2,1)S(1)} collective-permute-done((bf16[384,512]{1,0:T(8,128)(2,1)S(1)}, bf16[384,512]{1,0:T(8,128)(2,1)S(1)}, u32[]{:S(2)}, u32[]{:S(2)}) %collective-permute-start.11) | collective-permute-done | bytes 393248 | tf_op jit(solution)/shard_map/ppermute | solution.py:13
  130.1 8.3 %collective-permute-done.25 = bf16[384,512]{1,0:T(8,128)(2,1)S(1)} collective-permute-done((bf16[384,512]{1,0:T(8,128)(2,1)S(1)}, bf16[384,512]{1,0:T(8,128)(2,1)S(1)}, u32[]{:S(2)}, u32[]{:S(2)}) %collective-permute-start.25) | collective-permute-done | bytes 393248 | tf_op jit(solution)/shard_map/ppermute | solution.py:13
  139.6 1.3 convolution_add_fusion.1
  140.8 7.0 %collective-permute-start.27 = (f32[176,512]{1,0:T(8,128)}, f32[176,512]{1,0:T(8,128)S(1)}, u32[]{:S(2)}, u32[]{:S(2)}) collective-permute-start(f32[176,512]{1,0:T(8,128)} %convolution_add_fusion.1), channel_id=1, source_target_pairs={{0,8},{8,0},{1,9},{9,1},{2,10},{10,2},{3,11},{11,3},{4,12},{12,4},... | collective-permute-start | bytes 1081352 | tf_op jit(solution)/shard_map/ppermute | solution.py:13
  147.8 2.0 %fusion.9 = f32[176,512]{1,0:T(8,128)S(1)} fusion(bf16[1536,512]{1,0:T(8,128)(2,1)} %copy-done.1, bf16[176,6144]{1,0:T(8,128)(2,1)S(1)} %copy-done, s32[]{:T(128)S(6)} %add.347), kind=kOutput, calls=%fused_computation.21 | convolution fusion | flops 276824064 | bytes 2473988 | tf_op jit(solution)/shard_map/dot_general | solution.py:84
  (79 shorter events, 16.3 us)
Async XLA Ops:
  0.0 70.5 %copy-start = (bf16[176,6144]{1,0:T(8,128)(2,1)S(1)}, bf16[176,6144]{1,0:T(8,128)(2,1)}, u32[]{:S(2)}) copy-start(bf16[176,6144]{1,0:T(8,128)(2,1)} %param.7) | copy-start | bytes 6488068
  0.0 6.6 %copy-start.6 = (s32[192]{0:T(256)S(1)}, s32[192]{0:T(256)}, u32[]{:S(2)}) copy-start(s32[192]{0:T(256)} %param.9) | copy-start | bytes 2308
  0.0 22.4 %copy-start.5 = (s32[192]{0:T(256)S(1)}, s32[192]{0:T(256)}, u32[]{:S(2)}) copy-start(s32[192]{0:T(256)} %param.8) | copy-start | bytes 2308
  3.4 55.2 %collective-permute-start = (bf16[384,3072]{1,0:T(8,128)(2,1)}, bf16[384,3072]{1,0:T(8,128)(2,1)}, u32[]{:S(2)}, u32[]{:S(2)}) collective-permute-start(bf16[384,3072]{1,0:T(8,128)(2,1)} %dynamic-slice_bitcast_fusion), channel_id=1, source_target_pairs={{0,8},{8,0},{1,9},{9,1},{2,10},{10,2},{3,11},{11,3},{4,12},{12,4},... | collective-permute-start | bytes 7077896 | tf_op jit(solution)/shard_map/ppermute | solution.py:13
  48.6 10.0 %collective-permute-start.1 = (bf16[512,384]{1,0:T(8,128)(2,1)S(1)}, bf16[512,384]{1,0:T(8,128)(2,1)S(1)}, u32[]{:S(2)}, u32[]{:S(2)}) collective-permute-start(bf16[512,384]{1,0:T(8,128)(2,1)S(1)} %all_gather.3), channel_id=1, source_target_pairs={{0,8},{8,0},{1,9},{9,1},{2,10},{10,2},{3,11},{11,3},{4,12},{12,4},... | collective-permute-start | bytes 1179656 | tf_op jit(solution)/shard_map/ppermute | solution.py:13
  64.5 7.1 %copy-start.4 = (f32[1536,512]{1,0:T(8,128)}, f32[1536,512]{1,0:T(8,128)S(1)}, u32[]{:S(2)}) copy-start(f32[1536,512]{1,0:T(8,128)S(1)} %get-tuple-element.9) | copy-start | bytes 9437188
  65.7 12.3 %collective-permute-start.2 = (bf16[384,512]{1,0:T(8,128)(2,1)}, bf16[384,512]{1,0:T(8,128)(2,1)}, u32[]{:S(2)}, u32[]{:S(2)}) collective-permute-start(bf16[384,512]{1,0:T(8,128)(2,1)} %get-tuple-element.11), channel_id=1, source_target_pairs={{0,16},{16,32},{32,48},{48,0},{1,17},{17,33},{33,49},{49,1},{2,18}... | collective-permute-start | bytes 1179656 | tf_op jit(solution)/shard_map/ppermute | solution.py:13
  66.9 20.5 %collective-permute-start.3 = (bf16[384,512]{1,0:T(8,128)(2,1)}, bf16[384,512]{1,0:T(8,128)(2,1)}, u32[]{:S(2)}, u32[]{:S(2)}) collective-permute-start(bf16[384,512]{1,0:T(8,128)(2,1)} %get-tuple-element.13), channel_id=1, source_target_pairs={{0,32},{16,48},{32,0},{48,16},{1,33},{17,49},{33,1},{49,17},{2,34}... | collective-permute-start | bytes 1179656 | tf_op jit(solution)/shard_map/ppermute | solution.py:13
  69.4 20.8 %collective-permute-start.4 = (bf16[384,512]{1,0:T(8,128)(2,1)}, bf16[384,512]{1,0:T(8,128)(2,1)}, u32[]{:S(2)}, u32[]{:S(2)}) collective-permute-start(bf16[384,512]{1,0:T(8,128)(2,1)} %get-tuple-element.12), channel_id=1, source_target_pairs={{0,48},{16,0},{32,16},{48,32},{1,49},{17,1},{33,17},{49,33},{2,50}... | collective-permute-start | bytes 1179656 | tf_op jit(solution)/shard_map/ppermute | solution.py:13
  71.6 66.8 %collective-permute-start.26 = (bf16[176,3072]{1,0:T(8,128)(2,1)}, bf16[176,3072]{1,0:T(8,128)(2,1)S(1)}, u32[]{:S(2)}, u32[]{:S(2)}) collective-permute-start(bf16[176,3072]{1,0:T(8,128)(2,1)} %constant_dynamic-slice_fusion), channel_id=1, source_target_pairs={{0,8},{8,0},{1,9},{9,1},{2,10},{10,2},{3,11},{11,3},{4,12},{12,4},... | collective-permute-start | bytes 3244040 | tf_op jit(solution)/shard_map/ppermute | solution.py:13
  74.2 18.0 %collective-permute-start.14 = (bf16[384,512]{1,0:T(8,128)(2,1)S(1)}, bf16[384,512]{1,0:T(8,128)(2,1)S(1)}, u32[]{:S(2)}, u32[]{:S(2)}) collective-permute-start(bf16[384,512]{1,0:T(8,128)(2,1)S(1)} %get-tuple-element.14), channel_id=1, source_target_pairs={{0,64},{64,128},{128,192},{192,0},{1,65},{65,129},{129,193},{193,1... | collective-permute-start | bytes 1179656 | tf_op jit(solution)/shard_map/ppermute | solution.py:13
  78.0 17.9 %collective-permute-start.15 = (bf16[384,512]{1,0:T(8,128)(2,1)S(1)}, bf16[384,512]{1,0:T(8,128)(2,1)S(1)}, u32[]{:S(2)}, u32[]{:S(2)}) collective-permute-start(bf16[384,512]{1,0:T(8,128)(2,1)S(1)} %get-tuple-element.16), channel_id=1, source_target_pairs={{0,128},{64,192},{128,0},{192,64},{1,129},{65,193},{129,1},{193,65... | collective-permute-start | bytes 1179656 | tf_op jit(solution)/shard_map/ppermute | solution.py:13
  87.4 11.2 %collective-permute-start.16 = (bf16[384,512]{1,0:T(8,128)(2,1)S(1)}, bf16[384,512]{1,0:T(8,128)(2,1)S(1)}, u32[]{:S(2)}, u32[]{:S(2)}) collective-permute-start(bf16[384,512]{1,0:T(8,128)(2,1)S(1)} %get-tuple-element.15), channel_id=1, source_target_pairs={{0,192},{64,0},{128,64},{192,128},{1,193},{65,1},{129,65},{193,129... | collective-permute-start | bytes 1179656 | tf_op jit(solution)/shard_map/ppermute | solution.py:13
  91.9 8.8 %collective-permute-start.5 = (bf16[96,512]{1,0:T(8,128)(2,1)S(1)}, bf16[96,512]{1,0:T(8,128)(2,1)S(1)}, u32[]{:S(2)}, u32[]{:S(2)}) collective-permute-start(bf16[96,512]{1,0:T(8,128)(2,1)S(1)} %get-tuple-element.23), channel_id=1, source_target_pairs={{0,64},{64,128},{128,192},{192,0},{1,65},{65,129},{129,193},{193,1... | collective-permute-start | bytes 294920 | tf_op jit(solution)/shard_map/ppermute | solution.py:13
  92.2 11.0 %collective-permute-start.6 = (bf16[96,512]{1,0:T(8,128)(2,1)S(1)}, bf16[96,512]{1,0:T(8,128)(2,1)S(1)}, u32[]{:S(2)}, u32[]{:S(2)}) collective-permute-start(bf16[96,512]{1,0:T(8,128)(2,1)S(1)} %get-tuple-element.25), channel_id=1, source_target_pairs={{0,128},{64,192},{128,0},{192,64},{1,129},{65,193},{129,1},{193,65... | collective-permute-start | bytes 294920 | tf_op jit(solution)/shard_map/ppermute | solution.py:13
  95.9 8.5 %collective-permute-start.7 = (bf16[96,512]{1,0:T(8,128)(2,1)S(1)}, bf16[96,512]{1,0:T(8,128)(2,1)S(1)}, u32[]{:S(2)}, u32[]{:S(2)}) collective-permute-start(bf16[96,512]{1,0:T(8,128)(2,1)S(1)} %get-tuple-element.24), channel_id=1, source_target_pairs={{0,192},{64,0},{128,64},{192,128},{1,193},{65,1},{129,65},{193,129... | collective-permute-start | bytes 294920 | tf_op jit(solution)/shard_map/ppermute | solution.py:13
  100.0 6.2 %collective-permute-start.17 = (bf16[96,512]{1,0:T(8,128)(2,1)S(1)}, bf16[96,512]{1,0:T(8,128)(2,1)S(1)}, u32[]{:S(2)}, u32[]{:S(2)}) collective-permute-start(bf16[96,512]{1,0:T(8,128)(2,1)S(1)} %get-tuple-element.26), channel_id=1, source_target_pairs={{0,16},{16,32},{32,48},{48,0},{1,17},{17,33},{33,49},{49,1},{2,18}... | collective-permute-start | bytes 294920 | tf_op jit(solution)/shard_map/ppermute | solution.py:13
  100.7 8.6 %collective-permute-start.18 = (bf16[96,512]{1,0:T(8,128)(2,1)S(1)}, bf16[96,512]{1,0:T(8,128)(2,1)S(1)}, u32[]{:S(2)}, u32[]{:S(2)}) collective-permute-start(bf16[96,512]{1,0:T(8,128)(2,1)S(1)} %get-tuple-element.28), channel_id=1, source_target_pairs={{0,32},{16,48},{32,0},{48,16},{1,33},{17,49},{33,1},{49,17},{2,34}... | collective-permute-start | bytes 294920 | tf_op jit(solution)/shard_map/ppermute | solution.py:13
  103.2 6.6 %collective-permute-start.19 = (bf16[96,512]{1,0:T(8,128)(2,1)S(1)}, bf16[96,512]{1,0:T(8,128)(2,1)S(1)}, u32[]{:S(2)}, u32[]{:S(2)}) collective-permute-start(bf16[96,512]{1,0:T(8,128)(2,1)S(1)} %get-tuple-element.27), channel_id=1, source_target_pairs={{0,48},{16,0},{32,16},{48,32},{1,49},{17,1},{33,17},{49,33},{2,50}... | collective-permute-start | bytes 294920 | tf_op jit(solution)/shard_map/ppermute | solution.py:13
  104.5 6.3 %collective-permute-start.8 = (bf16[96,512]{1,0:T(8,128)(2,1)S(1)}, bf16[96,512]{1,0:T(8,128)(2,1)S(1)}, u32[]{:S(2)}, u32[]{:S(2)}) collective-permute-start(bf16[96,512]{1,0:T(8,128)(2,1)S(1)} %get-tuple-element.6), channel_id=1, source_target_pairs={{0,64},{64,128},{128,192},{192,0},{1,65},{65,129},{129,193},{193,1... | collective-permute-start | bytes 294920 | tf_op jit(solution)/shard_map/ppermute | solution.py:13
  106.2 6.2 %collective-permute-start.9 = (bf16[96,512]{1,0:T(8,128)(2,1)S(1)}, bf16[96,512]{1,0:T(8,128)(2,1)S(1)}, u32[]{:S(2)}, u32[]{:S(2)}) collective-permute-start(bf16[96,512]{1,0:T(8,128)(2,1)S(1)} %get-tuple-element.6), channel_id=1, source_target_pairs={{0,128},{64,192},{128,0},{192,64},{1,129},{65,193},{129,1},{193,65... | collective-permute-start | bytes 294920 | tf_op jit(solution)/shard_map/ppermute | solution.py:13
  109.3 4.7 %collective-permute-start.10 = (bf16[96,512]{1,0:T(8,128)(2,1)S(1)}, bf16[96,512]{1,0:T(8,128)(2,1)S(1)}, u32[]{:S(2)}, u32[]{:S(2)}) collective-permute-start(bf16[96,512]{1,0:T(8,128)(2,1)S(1)} %get-tuple-element.6), channel_id=1, source_target_pairs={{0,192},{64,0},{128,64},{192,128},{1,193},{65,1},{129,65},{193,129... | collective-permute-start | bytes 294920 | tf_op jit(solution)/shard_map/ppermute | solution.py:13
  109.8 4.8 %collective-permute-start.20 = (bf16[96,512]{1,0:T(8,128)(2,1)S(1)}, bf16[96,512]{1,0:T(8,128)(2,1)S(1)}, u32[]{:S(2)}, u32[]{:S(2)}) collective-permute-start(bf16[96,512]{1,0:T(8,128)(2,1)S(1)} %get-tuple-element.8), channel_id=1, source_target_pairs={{0,16},{16,32},{32,48},{48,0},{1,17},{17,33},{33,49},{49,1},{2,18}... | collective-permute-start | bytes 294920 | tf_op jit(solution)/shard_map/ppermute | solution.py:13
  110.8 5.3 %collective-permute-start.21 = (bf16[96,512]{1,0:T(8,128)(2,1)S(1)}, bf16[96,512]{1,0:T(8,128)(2,1)S(1)}, u32[]{:S(2)}, u32[]{:S(2)}) collective-permute-start(bf16[96,512]{1,0:T(8,128)(2,1)S(1)} %get-tuple-element.8), channel_id=1, source_target_pairs={{0,32},{16,48},{32,0},{48,16},{1,33},{17,49},{33,1},{49,17},{2,34}... | collective-permute-start | bytes 294920 | tf_op jit(solution)/shard_map/ppermute | solution.py:13
  112.4 4.2 %collective-permute-start.22 = (bf16[96,512]{1,0:T(8,128)(2,1)S(1)}, bf16[96,512]{1,0:T(8,128)(2,1)S(1)}, u32[]{:S(2)}, u32[]{:S(2)}) collective-permute-start(bf16[96,512]{1,0:T(8,128)(2,1)S(1)} %get-tuple-element.8), channel_id=1, source_target_pairs={{0,48},{16,0},{32,16},{48,32},{1,49},{17,1},{33,17},{49,33},{2,50}... | collective-permute-start | bytes 294920 | tf_op jit(solution)/shard_map/ppermute | solution.py:13
  114.1 15.3 %collective-permute-start.11 = (bf16[384,512]{1,0:T(8,128)(2,1)S(1)}, bf16[384,512]{1,0:T(8,128)(2,1)S(1)}, u32[]{:S(2)}, u32[]{:S(2)}) collective-permute-start(bf16[384,512]{1,0:T(8,128)(2,1)S(1)} %constant_dynamic-update-slice_fusion.12), channel_id=1, source_target_pairs={{0,16},{16,32},{32,48},{48,0},{1,17},{17,33},{33,49},{49,1},{2,18}... | collective-permute-start | bytes 1179656 | tf_op jit(solution)/shard_map/ppermute | solution.py:13
  114.6 15.3 %collective-permute-start.12 = (bf16[384,512]{1,0:T(8,128)(2,1)S(1)}, bf16[384,512]{1,0:T(8,128)(2,1)S(1)}, u32[]{:S(2)}, u32[]{:S(2)}) collective-permute-start(bf16[384,512]{1,0:T(8,128)(2,1)S(1)} %constant_dynamic-update-slice_fusion.12), channel_id=1, source_target_pairs={{0,32},{16,48},{32,0},{48,16},{1,33},{17,49},{33,1},{49,17},{2,34}... | collective-permute-start | bytes 1179656 | tf_op jit(solution)/shard_map/ppermute | solution.py:13
  116.5 13.4 %collective-permute-start.23 = (bf16[384,512]{1,0:T(8,128)(2,1)S(1)}, bf16[384,512]{1,0:T(8,128)(2,1)S(1)}, u32[]{:S(2)}, u32[]{:S(2)}) collective-permute-start(bf16[384,512]{1,0:T(8,128)(2,1)S(1)} %constant_dynamic-update-slice_fusion.4), channel_id=1, source_target_pairs={{0,64},{64,128},{128,192},{192,0},{1,65},{65,129},{129,193},{193,1... | collective-permute-start | bytes 1179656 | tf_op jit(solution)/shard_map/ppermute | solution.py:13
  117.6 12.4 %collective-permute-start.24 = (bf16[384,512]{1,0:T(8,128)(2,1)S(1)}, bf16[384,512]{1,0:T(8,128)(2,1)S(1)}, u32[]{:S(2)}, u32[]{:S(2)}) collective-permute-start(bf16[384,512]{1,0:T(8,128)(2,1)S(1)} %constant_dynamic-update-slice_fusion.4), channel_id=1, source_target_pairs={{0,128},{64,192},{128,0},{192,64},{1,129},{65,193},{129,1},{193,65... | collective-permute-start | bytes 1179656 | tf_op jit(solution)/shard_map/ppermute | solution.py:13
  129.3 9.0 %collective-permute-start.25 = (bf16[384,512]{1,0:T(8,128)(2,1)S(1)}, bf16[384,512]{1,0:T(8,128)(2,1)S(1)}, u32[]{:S(2)}, u32[]{:S(2)}) collective-permute-start(bf16[384,512]{1,0:T(8,128)(2,1)S(1)} %constant_dynamic-update-slice_fusion.4), channel_id=1, source_target_pairs={{0,192},{64,0},{128,64},{192,128},{1,193},{65,1},{129,65},{193,129... | collective-permute-start | bytes 1179656 | tf_op jit(solution)/shard_map/ppermute | solution.py:13
  129.9 8.9 %collective-permute-start.13 = (bf16[384,512]{1,0:T(8,128)(2,1)S(1)}, bf16[384,512]{1,0:T(8,128)(2,1)S(1)}, u32[]{:S(2)}, u32[]{:S(2)}) collective-permute-start(bf16[384,512]{1,0:T(8,128)(2,1)S(1)} %constant_dynamic-update-slice_fusion.12), channel_id=1, source_target_pairs={{0,48},{16,0},{32,16},{48,32},{1,49},{17,1},{33,17},{49,33},{2,50}... | collective-permute-start | bytes 1179656 | tf_op jit(solution)/shard_map/ppermute | solution.py:13
  140.8 8.9 %collective-permute-start.27 = (f32[176,512]{1,0:T(8,128)}, f32[176,512]{1,0:T(8,128)S(1)}, u32[]{:S(2)}, u32[]{:S(2)}) collective-permute-start(f32[176,512]{1,0:T(8,128)} %convolution_add_fusion.1), channel_id=1, source_target_pairs={{0,8},{8,0},{1,9},{9,1},{2,10},{10,2},{3,11},{11,3},{4,12},{12,4},... | collective-permute-start | bytes 1081352 | tf_op jit(solution)/shard_map/ppermute | solution.py:13
  (3 other events, 4.4 us)

commit v2 on v0

v2 whole, which is shorter than its diff:
```python
import jax
import jax.numpy as jnp
from jax import lax
from jax.experimental import pallas as pl
from jax.experimental.pallas import tpu as pltpu
from jax.sharding import Mesh
from jax.sharding import PartitionSpec as P

N, C, Z = 4, 2, 8
PAIR = ("y", "x", "core")
ORDER = (2, 1, 3)
F32, BF16 = jnp.float32, jnp.bfloat16


def after(value, *others):
    return lax.optimization_barrier((value, *others))[0]


def hop(value, leg, step):
    pairs = []
    for y in range(N):
        for x in range(N):
            for core in range(C):
                to_y, to_x = (y, (x + step) % N) if core == leg else ((y + step) % N, x)
                pairs.append(((y * N + x) * C + core, (to_y * N + to_x) * C + core))
    return lax.ppermute(value, PAIR, pairs)


def exchange(value, leg, mask):
    pairs = []
    for y in range(N):
        for x in range(N):
            for core in range(C):
                to_y, to_x = (y, x ^ mask) if core == leg else (y ^ mask, x)
                pairs.append(((y * N + x) * C + core, (to_y * N + to_x) * C + core))
    return lax.ppermute(value, PAIR, pairs)


def swap(value):
    return lax.ppermute(value, "core", [(0, 1), (1, 0)])


def layers(value, step):
    pairs = [(z, (z - step) % Z) for z in range(Z)] + [(Z + z, Z + (z + step) % Z) for z in range(Z)]
    return lax.ppermute(value, ("core", "z"), pairs)


def pick_columns(slots, screen, coef, width, first, second):
    rows = coef.shape[0]
    count = slots.shape[0] // (N * N * C)
    tile = 2 * width

    def kernel(place_ref, slots_ref, screen_ref, coef_ref, out):
        lane = lax.broadcasted_iota(jnp.int32, (rows, tile), 1)
        for p in range(count):
            halves = []
            for side in range(2):
                run, s = divmod(2 * p + side, count)
                block = slots_ref[place_ref[run] * count + s]
                at = pl.multiple_of(block // 2 * tile, tile)
                value = coef_ref[:, pl.ds(at, tile)].astype(F32) * screen_ref[block].astype(F32)
                halves.append(jnp.where(block % 2 != side, pltpu.roll(value, width, 1), value))
            out[:, p * tile : (p + 1) * tile] = jnp.where(lane < width, halves[0], halves[1]).astype(BF16)

    smem, vmem = pl.BlockSpec(memory_space=pltpu.SMEM), pl.BlockSpec(memory_space=pltpu.VMEM)
    return pl.pallas_call(
        kernel,
        out_shape=jax.ShapeDtypeStruct((rows, 2 * count * width), BF16),
        in_specs=[smem, smem, smem, vmem],
        out_specs=vmem,
        compiler_params=pltpu.CompilerParams(vmem_limit_bytes=20 << 20),
        name="pick",
    )(jnp.stack([first, second]).astype(jnp.int32), slots, screen, coef)


def turned(parts, places, height):
    whole = jnp.concatenate(parts, axis=0)
    rows = whole.shape[0]
    start = places % (rows // height) * height
    return lax.dynamic_slice_in_dim(jnp.concatenate([whole, whole], axis=0), start, rows, 0)


def gather_layers(own, core, z, *ready):
    rows, cols = own.shape
    next_one = layers(own, 1)
    next_two = layers(own, 2)
    pair = layers(after(jnp.concatenate([next_one, next_two], axis=0), *ready), 2)
    got = jnp.concatenate([next_one, next_two, pair], axis=0)
    other = swap(got)
    other = jnp.concatenate([other[:, cols // 2 :], other[:, : cols // 2]], axis=1)
    up, down = jnp.where(core == 0, got, other), jnp.where(core == 0, other, got)
    up, down = up.reshape(4, rows, cols), down.reshape(4, rows, cols)
    return turned([down[0], own, up[0], up[1], up[2], up[3], down[2], down[1]], 1 - z, rows)


def block_of(value, index, width, axis):
    return lax.dynamic_slice_in_dim(value, index * width, width, axis)


def add(parts):
    total = parts[0].astype(F32)
    for piece in parts[1:]:
        total = total + piece.astype(F32)
    return total


def shards(half_ints, pair_coef, mo_virtual, screen, slot_block):
    y, x, core, z = (lax.axis_index(a) for a in ("y", "x", "core", "z"))
    first, second = jnp.where(core == 0, x, y), jnp.where(core == 0, y, x)
    chip = y * N + x
    width = half_ints.shape[2] // (C * N)

    ints_taken = swap(half_ints)
    virt_taken = swap(mo_virtual)
    slot_width = pair_coef.shape[1] // screen.shape[0]
    own = pick_columns(slot_block, screen, pair_coef, slot_width, chip * C + core, chip * C + 1 - core)

    def ints_block(ints, step):
        return block_of(ints[0], N * core + (first + step) % N, width, 1)

    def virt_block(step):
        at = N * core + (first - step) % N
        return jnp.concatenate([block_of(mo_virtual, at, width, 1), block_of(virt_taken, at, width, 1)], axis=0)

    virt = [virt_block(0)] + [hop(virt_block(s), 0, N - s) for s in (1, 2, 3)]
    chosen = gather_layers(own, core, z, ints_taken)
    chosen = after(chosen, virt[1], virt[3])

    def product(step, chosen):
        both = jnp.concatenate([ints_block(half_ints, step), ints_block(ints_taken, step)], axis=0)
        return jnp.dot(chosen, both, preferred_element_type=F32)

    got = [hop(product(s, chosen).astype(BF16), 0, s) for s in ORDER]
    kept = lax.optimization_barrier(product(0, after(chosen, virt[2])))
    total = add([kept, *got])
    half = total.shape[0] // 2
    ends = [total[:half], total[half:]]
    for masks in ((1, 3), (3, 1)):
        ends = [part + exchange(part.astype(BF16), 1, mask).astype(F32) for part, mask in zip(ends, masks)]
    ends = [part.astype(BF16) for part in ends]
    summed = jnp.concatenate(ends, axis=0)

    def fold(step):
        return lax.dot_general(virt[step], summed, (((1,), (1,)), ((), ())), preferred_element_type=F32)

    got = [hop(fold(s).astype(BF16), 0, s) for s in ORDER]
    both = add([lax.optimization_barrier(fold(0)), *got])
    rows = mo_virtual.shape[0]
    out = (both[:rows] + swap(both[rows:])).astype(BF16)
    return out[:, None, :]


def solution(mesh):
    split = Mesh(mesh.devices.reshape(N, N, C, Z), ("y", "x", "core", "z"))
    placed = (P("z", PAIR, None), P("z", None), P(PAIR, None), P(), P())
    return jax.shard_map(
        shards, mesh=split, in_specs=placed, out_specs=P(PAIR, "z", None), check_vma=False
    )
```

time: 1390 us -> 97.4 us (0.07)
  blocking collectives: 1090 us -> 0 us
  waiting for transfers between devices: 193 us -> 43.5 us
  local copies, waits for them, and re-layouts: 60.1 us -> 7.39 us
  starting transfers between devices: 0.04 us -> 38 us
    unnamed x1 -> x0, blocking collectives: 1090 us -> none
    all_gather x2 -> x0, waiting for transfers between devices: 192 us -> none  [the longest x1 135 us: shards(): coef_all = lax.all_gather(pair_coef, 'occ', axis=0, tiled=True)]
    ppermute x0 -> x20, waiting for transfers between devices: none -> 43.5 us  [the longest x9 21.7 us: hop(): return lax.ppermute(value, PAIR, pairs)]
    ppermute x0 -> x20, starting transfers between devices: none -> 38 us  [the longest x9 22.1 us: hop(): return lax.ppermute(value, PAIR, pairs)]
    transpose x1 -> x0, local copies, waits for them, and re-layouts: 27 us -> none  [shards(): jnp.einsum('jq,iqn->nij', local_cols, half_ints, preferred_element_type=j...]
    all_gather x1 -> x0, local copies, waits for them, and re-layouts: 16.6 us -> none  [shards(): coef_all = lax.all_gather(pair_coef, 'occ', axis=0, tiled=True)]
  transfers between devices with their start and end apart: 2 -> 20, of which waited for: 2 -> 13; matrix products, arithmetic and copies ran while one was open for 0% -> 9% of each run, Pallas kernels for 0% -> 1%
where the time goes in v2:
time: 97.4 us; the launch traced here: 97.2 us
  waiting for transfers between devices  43.5 us (45%)
  starting transfers between devices  38 us (39%)
  local copies, waits for them, and re-layouts  7.39 us (8%)
  matrix products  5.04 us (5%)
  other arithmetic  2.25 us (2%)
    ppermute x9, starting transfers between devices, hop(): return lax.ppermute(value, PAIR, pairs)  22.1 us
    ppermute x9, waiting for transfers between devices, hop(): return lax.ppermute(value, PAIR, pairs)  21.7 us
    ppermute x4, waiting for transfers between devices, exchange(): return lax.ppermute(value, PAIR, pairs)  12.9 us
    ppermute x3, waiting for transfers between devices, layers(): return lax.ppermute(value, ('core', 'z'), pairs)  7.56 us
    ppermute x4, starting transfers between devices, swap(): return lax.ppermute(value, 'core', [(0, 1), (1, 0)])  7.54 us
    ppermute x4, starting transfers between devices, exchange(): return lax.ppermute(value, PAIR, pairs)  5.31 us
    dynamic_slice x4, local copies, waits for them, and re-layouts, block_of(): return lax.dynamic_slice_in_dim(value, index * width, width, axis)  3.9 us
    unnamed x17, local copies, waits for them, and re-layouts  3.26 us
  transfers between devices with their start and end apart: 20, of which 13 were waited for; matrix products, arithmetic and copies ran while one was open for 9% of the time, Pallas kernels for 1%

profile of v2, /device:TPU:1, one launch (start us, length us, event | category | flops | bytes accessed | tf_op | source)
XLA Modules:
  0.0 97.2 jit_solution(14131532811302999355)
XLA Ops:
  0.0 3.2 %collective-permute-start.3 = (bf16[1,384,6144]{2,1,0:T(8,128)(2,1)}, bf16[1,384,6144]{2,1,0:T(8,128)(2,1)}, u32[]{:S(2)}, u32[]{:S(2)}) collective-permute-start(bf16[1,384,6144]{2,1,0:T(8,128)(2,1)} %param.5), channel_id=1, source_target_pairs={{0,8},{8,0},{1,9},{9,1},{2,10},{10,2},{3,11},{11,3},{4,12},{12,4},... | collective-permute-start | bytes 14155784 | tf_op jit(solution)/shard_map/ppermute | solution.py:40
  3.3 1.4 %copy-done = bf16[64,12288]{1,0:T(8,128)(2,1)S(1)} copy-done((bf16[64,12288]{1,0:T(8,128)(2,1)S(1)}, bf16[64,12288]{1,0:T(8,128)(2,1)}, u32[]{:S(2)}) %copy-start) | copy-done | bytes 1572888
  6.9 2.9 %collective-permute-start.2 = (bf16[64,768]{1,0:T(8,128)(2,1)S(1)}, bf16[64,768]{1,0:T(8,128)(2,1)S(1)}, u32[]{:S(2)}, u32[]{:S(2)}) collective-permute-start(bf16[64,768]{1,0:T(8,128)(2,1)S(1)} %pick.1), channel_id=1, source_target_pairs={{0,6},{1,7},{2,0},{3,1},{4,2},{5,3},{6,4},{7,5},{8,10},{9,11},{10,... | collective-permute-start | bytes 294920 | tf_op jit(solution)/shard_map/ppermute | solution.py:45
  9.8 1.9 %dynamic-slice_bitcast_fusion.5 = (bf16[384,768]{1,0:T(8,128)(2,1)S(1)}, bf16[384,768]{1,0:T(8,128)(2,1)S(1)}, bf16[384,768]{1,0:T(8,128)(2,1)S(1)}, bf16[384,768]{1,0:T(8,128)(2,1)S(1)}) fusion(bf16[1,384,6144]{2,1,0:T(8,128)(2,1)} %param.5, s32[]{:T(128)S(6)} %select_n.108, s32[]{:T(128)S(6)} %select_n.95, s32[]{:T(128)S(6)} %select_n.112, s32[]{:T(128)S(6)} %select_n.110), kind=kLoop, calls=%fused_computation.33 | loop fusion | bytes 4718608 | tf_op jit(solution)/shard_map/dynamic_slice | solution.py:97
  12.8 2.9 %collective-permute-done.2 = bf16[64,768]{1,0:T(8,128)(2,1)S(1)} collective-permute-done((bf16[64,768]{1,0:T(8,128)(2,1)S(1)}, bf16[64,768]{1,0:T(8,128)(2,1)S(1)}, u32[]{:S(2)}, u32[]{:S(2)}) %collective-permute-start.2) | collective-permute-done | bytes 98336 | tf_op jit(solution)/shard_map/ppermute | solution.py:45
  16.0 2.8 %collective-permute-start.6 = (bf16[352,768]{1,0:T(8,128)(2,1)S(1)}, bf16[352,768]{1,0:T(8,128)(2,1)S(1)}, u32[]{:S(2)}, u32[]{:S(2)}) collective-permute-start(bf16[352,768]{1,0:T(8,128)(2,1)S(1)} %pad_maximum_fusion.1), channel_id=1, source_target_pairs={{0,48},{8,200},{16,0},{24,216},{32,16},{40,232},{48,32},{56,248},{... | collective-permute-start | bytes 1622024 | tf_op jit(solution)/shard_map/ppermute | solution.py:26
  18.8 4.2 %collective-permute-done.4 = bf16[128,768]{1,0:T(8,128)(2,1)S(1)} collective-permute-done((bf16[128,768]{1,0:T(8,128)(2,1)S(1)}, bf16[128,768]{1,0:T(8,128)(2,1)S(1)}, u32[]{:S(2)}, u32[]{:S(2)}) %collective-permute-start.4) | collective-permute-done | bytes 196640 | tf_op jit(solution)/shard_map/ppermute | solution.py:45
  23.0 1.8 %collective-permute-start.5 = (bf16[256,768]{1,0:T(8,128)(2,1)S(1)}, bf16[256,768]{1,0:T(8,128)(2,1)S(1)}, u32[]{:S(2)}, u32[]{:S(2)}) collective-permute-start(bf16[256,768]{1,0:T(8,128)(2,1)S(1)} %constant_dynamic-update-slice_fusion), channel_id=1, source_target_pairs={{0,8},{8,0},{1,9},{9,1},{2,10},{10,2},{3,11},{11,3},{4,12},{12,4},... | collective-permute-start | bytes 1179656 | tf_op jit(solution)/shard_map/ppermute | solution.py:40
  24.9 1.4 %collective-permute-start.7 = (bf16[352,768]{1,0:T(8,128)(2,1)S(1)}, bf16[352,768]{1,0:T(8,128)(2,1)S(1)}, u32[]{:S(2)}, u32[]{:S(2)}) collective-permute-start(bf16[352,768]{1,0:T(8,128)(2,1)S(1)} %pad_maximum_fusion.2), channel_id=1, source_target_pairs={{0,16},{8,72},{16,32},{24,88},{32,48},{40,104},{48,0},{56,120},{64... | collective-permute-start | bytes 1622024 | tf_op jit(solution)/shard_map/ppermute | solution.py:26
  26.3 2.7 %collective-permute-start.8 = (bf16[352,768]{1,0:T(8,128)(2,1)S(1)}, bf16[352,768]{1,0:T(8,128)(2,1)S(1)}, u32[]{:S(2)}, u32[]{:S(2)}) collective-permute-start(bf16[352,768]{1,0:T(8,128)(2,1)S(1)} %pad_maximum_fusion.3), channel_id=1, source_target_pairs={{0,32},{8,136},{16,48},{24,152},{32,0},{40,168},{48,16},{56,184},{... | collective-permute-start | bytes 1622024 | tf_op jit(solution)/shard_map/ppermute | solution.py:26
  29.0 1.8 %dynamic-slice_bitcast_fusion.4 = (bf16[384,768]{1,0:T(8,128)(2,1)S(1)}, bf16[384,768]{1,0:T(8,128)(2,1)S(1)}, bf16[384,768]{1,0:T(8,128)(2,1)S(1)}, bf16[384,768]{1,0:T(8,128)(2,1)S(1)}) fusion(bf16[1,384,6144]{2,1,0:T(8,128)(2,1)} %collective-permute-done.3, s32[]{:T(128)S(6)} %select_n.108, s32[]{:T(128)S(6)} %select_n.112, s32[]{:T(128)S(6)} %select_n.110, ...), kind=kLoop, calls=%fused_computation.32 | loop fusion | bytes 4718608 | tf_op jit(solution)/shard_map/dynamic_slice | solution.py:97
  31.4 3.4 %collective-permute-done.7 = bf16[352,768]{1,0:T(8,128)(2,1)S(1)} collective-permute-done((bf16[352,768]{1,0:T(8,128)(2,1)S(1)}, bf16[352,768]{1,0:T(8,128)(2,1)S(1)}, u32[]{:S(2)}, u32[]{:S(2)}) %collective-permute-start.7) | collective-permute-done | bytes 540704 | tf_op jit(solution)/shard_map/ppermute | solution.py:26
  34.7 0.8 convolution_convert_fusion.2
  35.5 7.5 %collective-permute-start.9 = (bf16[512,768]{1,0:T(8,128)(2,1)S(1)}, bf16[512,768]{1,0:T(8,128)(2,1)S(1)}, u32[]{:S(2)}, u32[]{:S(2)}) collective-permute-start(bf16[512,768]{1,0:T(8,128)(2,1)S(1)} %convolution_convert_fusion.2), channel_id=1, source_target_pairs={{0,32},{8,136},{16,48},{24,152},{32,0},{40,168},{48,16},{56,184},{... | collective-permute-start | bytes 2359304 | tf_op jit(solution)/shard_map/ppermute | solution.py:26
  43.9 0.8 convolution_convert_fusion
  44.7 2.9 %collective-permute-start.11 = (bf16[512,768]{1,0:T(8,128)(2,1)S(1)}, bf16[512,768]{1,0:T(8,128)(2,1)S(1)}, u32[]{:S(2)}, u32[]{:S(2)}) collective-permute-start(bf16[512,768]{1,0:T(8,128)(2,1)S(1)} %convolution_convert_fusion), channel_id=1, source_target_pairs={{0,48},{8,200},{16,0},{24,216},{32,16},{40,232},{48,32},{56,248},{... | collective-permute-start | bytes 2359304 | tf_op jit(solution)/shard_map/ppermute | solution.py:26
  47.6 0.8 fusion
  48.4 4.1 %collective-permute-done.9 = bf16[512,768]{1,0:T(8,128)(2,1)S(1)} collective-permute-done((bf16[512,768]{1,0:T(8,128)(2,1)S(1)}, bf16[512,768]{1,0:T(8,128)(2,1)S(1)}, u32[]{:S(2)}, u32[]{:S(2)}) %collective-permute-start.9) | collective-permute-done | bytes 786464 | tf_op jit(solution)/shard_map/ppermute | solution.py:26
  52.5 8.3 %collective-permute-done.10 = bf16[512,768]{1,0:T(8,128)(2,1)S(1)} collective-permute-done((bf16[512,768]{1,0:T(8,128)(2,1)S(1)}, bf16[512,768]{1,0:T(8,128)(2,1)S(1)}, u32[]{:S(2)}, u32[]{:S(2)}) %collective-permute-start.10) | collective-permute-done | bytes 786464 | tf_op jit(solution)/shard_map/ppermute | solution.py:26
  61.2 1.0 %collective-permute-start.12 = (bf16[256,768]{1,0:T(8,128)(2,1)S(1)}, bf16[256,768]{1,0:T(8,128)(2,1)S(1)}, u32[]{:S(2)}, u32[]{:S(2)}) collective-permute-start(bf16[256,768]{1,0:T(8,128)(2,1)S(1)} %get-tuple-element.31), channel_id=1, source_target_pairs={{0,64},{8,24},{16,80},{24,8},{32,96},{40,56},{48,112},{56,40},{64,... | collective-permute-start | bytes 1179656 | tf_op jit(solution)/shard_map/ppermute | solution.py:36
  62.2 2.1 %collective-permute-start.14 = (bf16[256,768]{1,0:T(8,128)(2,1)S(1)}, bf16[256,768]{1,0:T(8,128)(2,1)S(1)}, u32[]{:S(2)}, u32[]{:S(2)}) collective-permute-start(bf16[256,768]{1,0:T(8,128)(2,1)S(1)} %get-tuple-element.32), channel_id=1, source_target_pairs={{0,192},{8,56},{16,208},{24,40},{32,224},{40,24},{48,240},{56,8},{... | collective-permute-start | bytes 1179656 | tf_op jit(solution)/shard_map/ppermute | solution.py:36
  64.4 3.9 %collective-permute-done.12 = bf16[256,768]{1,0:T(8,128)(2,1)S(1)} collective-permute-done((bf16[256,768]{1,0:T(8,128)(2,1)S(1)}, bf16[256,768]{1,0:T(8,128)(2,1)S(1)}, u32[]{:S(2)}, u32[]{:S(2)}) %collective-permute-start.12) | collective-permute-done | bytes 393248 | tf_op jit(solution)/shard_map/ppermute | solution.py:36
  68.2 2.1 %collective-permute-done.14 = bf16[256,768]{1,0:T(8,128)(2,1)S(1)} collective-permute-done((bf16[256,768]{1,0:T(8,128)(2,1)S(1)}, bf16[256,768]{1,0:T(8,128)(2,1)S(1)}, u32[]{:S(2)}, u32[]{:S(2)}) %collective-permute-start.14) | collective-permute-done | bytes 393248 | tf_op jit(solution)/shard_map/ppermute | solution.py:36
  70.6 2.2 %collective-permute-start.13 = (bf16[256,768]{1,0:T(8,128)(2,1)S(1)}, bf16[256,768]{1,0:T(8,128)(2,1)S(1)}, u32[]{:S(2)}, u32[]{:S(2)}) collective-permute-start(bf16[256,768]{1,0:T(8,128)(2,1)S(1)} %get-tuple-element.29), channel_id=1, source_target_pairs={{0,192},{8,56},{16,208},{24,40},{32,224},{40,24},{48,240},{56,8},{... | collective-permute-start | bytes 1179656 | tf_op jit(solution)/shard_map/ppermute | solution.py:36
  72.8 6.0 %collective-permute-done.13 = bf16[256,768]{1,0:T(8,128)(2,1)S(1)} collective-permute-done((bf16[256,768]{1,0:T(8,128)(2,1)S(1)}, bf16[256,768]{1,0:T(8,128)(2,1)S(1)}, u32[]{:S(2)}, u32[]{:S(2)}) %collective-permute-start.13) | collective-permute-done | bytes 393248 | tf_op jit(solution)/shard_map/ppermute | solution.py:36
  78.8 0.9 collective-permute-done.15
  80.5 1.8 %collective-permute-start.16 = (bf16[352,512]{1,0:T(8,128)(2,1)S(1)}, bf16[352,512]{1,0:T(8,128)(2,1)S(1)}, u32[]{:S(2)}, u32[]{:S(2)}) collective-permute-start(bf16[352,512]{1,0:T(8,128)(2,1)S(1)} %convolution_convert_fusion.5), channel_id=1, source_target_pairs={{0,32},{8,136},{16,48},{24,152},{32,0},{40,168},{48,16},{56,184},{... | collective-permute-start | bytes 1081352 | tf_op jit(solution)/shard_map/ppermute | solution.py:26
  83.4 2.7 %collective-permute-start.18 = (bf16[352,512]{1,0:T(8,128)(2,1)S(1)}, bf16[352,512]{1,0:T(8,128)(2,1)S(1)}, u32[]{:S(2)}, u32[]{:S(2)}) collective-permute-start(bf16[352,512]{1,0:T(8,128)(2,1)S(1)} %convolution_convert_fusion.3), channel_id=1, source_target_pairs={{0,48},{8,200},{16,0},{24,216},{32,16},{40,232},{48,32},{56,248},{... | collective-permute-start | bytes 1081352 | tf_op jit(solution)/shard_map/ppermute | solution.py:26
  86.6 2.1 %collective-permute-done.16 = bf16[352,512]{1,0:T(8,128)(2,1)S(1)} collective-permute-done((bf16[352,512]{1,0:T(8,128)(2,1)S(1)}, bf16[352,512]{1,0:T(8,128)(2,1)S(1)}, u32[]{:S(2)}, u32[]{:S(2)}) %collective-permute-start.16) | collective-permute-done | bytes 360480 | tf_op jit(solution)/shard_map/ppermute | solution.py:26
  88.7 3.8 %collective-permute-done.17 = bf16[352,512]{1,0:T(8,128)(2,1)S(1)} collective-permute-done((bf16[352,512]{1,0:T(8,128)(2,1)S(1)}, bf16[352,512]{1,0:T(8,128)(2,1)S(1)}, u32[]{:S(2)}, u32[]{:S(2)}) %collective-permute-start.17) | collective-permute-done | bytes 360480 | tf_op jit(solution)/shard_map/ppermute | solution.py:26
  92.7 2.5 %collective-permute-start.19 = (f32[176,512]{1,0:T(8,128)S(1)}, f32[176,512]{1,0:T(8,128)S(1)}, u32[]{:S(2)}, u32[]{:S(2)}) collective-permute-start(f32[176,512]{1,0:T(8,128)S(1)} %slice.57), channel_id=1, source_target_pairs={{0,8},{8,0},{1,9},{9,1},{2,10},{10,2},{3,11},{11,3},{4,12},{12,4},... | collective-permute-start | bytes 1081352 | tf_op jit(solution)/shard_map/ppermute | solution.py:40
  95.2 1.3 %collective-permute-done.19 = f32[176,512]{1,0:T(8,128)S(1)} collective-permute-done((f32[176,512]{1,0:T(8,128)S(1)}, f32[176,512]{1,0:T(8,128)S(1)}, u32[]{:S(2)}, u32[]{:S(2)}) %collective-permute-start.19) | collective-permute-done | bytes 360480 | tf_op jit(solution)/shard_map/ppermute | solution.py:40
  (57 shorter events, 8.9 us)
Async XLA Ops:
  0.0 15.7 %collective-permute-start.3 = (bf16[1,384,6144]{2,1,0:T(8,128)(2,1)}, bf16[1,384,6144]{2,1,0:T(8,128)(2,1)}, u32[]{:S(2)}, u32[]{:S(2)}) collective-permute-start(bf16[1,384,6144]{2,1,0:T(8,128)(2,1)} %param.5), channel_id=1, source_target_pairs={{0,8},{8,0},{1,9},{9,1},{2,10},{10,2},{3,11},{11,3},{4,12},{12,4},... | collective-permute-start | bytes 14155784 | tf_op jit(solution)/shard_map/ppermute | solution.py:40
  3.2 12.6 %collective-permute-start = (bf16[176,6144]{1,0:T(8,128)(2,1)}, bf16[176,6144]{1,0:T(8,128)(2,1)S(1)}, u32[]{:S(2)}, u32[]{:S(2)}) collective-permute-start(bf16[176,6144]{1,0:T(8,128)(2,1)} %param.7), channel_id=1, source_target_pairs={{0,8},{8,0},{1,9},{9,1},{2,10},{10,2},{3,11},{11,3},{4,12},{12,4},... | collective-permute-start | bytes 6488072 | tf_op jit(solution)/shard_map/ppermute | solution.py:40
  3.3 1.4 %copy-start = (bf16[64,12288]{1,0:T(8,128)(2,1)S(1)}, bf16[64,12288]{1,0:T(8,128)(2,1)}, u32[]{:S(2)}) copy-start(bf16[64,12288]{1,0:T(8,128)(2,1)} %coef_ref.1) | copy-start | bytes 4718596
  4.7 0.7 copy-start.1
  5.4 0.7 copy-start.2
  6.8 5.9 %collective-permute-start.1 = (bf16[64,768]{1,0:T(8,128)(2,1)S(1)}, bf16[64,768]{1,0:T(8,128)(2,1)S(1)}, u32[]{:S(2)}, u32[]{:S(2)}) collective-permute-start(bf16[64,768]{1,0:T(8,128)(2,1)S(1)} %pick.1), channel_id=1, source_target_pairs={{0,7},{1,0},{2,1},{3,2},{4,3},{5,4},{6,5},{7,6},{8,9},{9,10},{10,1... | collective-permute-start | bytes 294920 | tf_op jit(solution)/shard_map/ppermute | solution.py:45
  6.9 8.7 %collective-permute-start.2 = (bf16[64,768]{1,0:T(8,128)(2,1)S(1)}, bf16[64,768]{1,0:T(8,128)(2,1)S(1)}, u32[]{:S(2)}, u32[]{:S(2)}) collective-permute-start(bf16[64,768]{1,0:T(8,128)(2,1)S(1)} %pick.1), channel_id=1, source_target_pairs={{0,6},{1,7},{2,0},{3,1},{4,2},{5,3},{6,4},{7,5},{8,10},{9,11},{10,... | collective-permute-start | bytes 294920 | tf_op jit(solution)/shard_map/ppermute | solution.py:45
  9.8 2.3 %copy-start.3 = (bf16[176,6144]{1,0:T(8,128)(2,1)S(1)}, bf16[176,6144]{1,0:T(8,128)(2,1)}, u32[]{:S(2)}) copy-start(bf16[176,6144]{1,0:T(8,128)(2,1)} %param.7) | copy-start | bytes 6488068
  15.7 7.3 %collective-permute-start.4 = (bf16[128,768]{1,0:T(8,128)(2,1)S(1)}, bf16[128,768]{1,0:T(8,128)(2,1)S(1)}, u32[]{:S(2)}, u32[]{:S(2)}) collective-permute-start(bf16[128,768]{1,0:T(8,128)(2,1)S(1)} %pad_maximum_fusion.5), channel_id=1, source_target_pairs={{0,6},{1,7},{2,0},{3,1},{4,2},{5,3},{6,4},{7,5},{8,10},{9,11},{10,... | collective-permute-start | bytes 589832 | tf_op jit(solution)/shard_map/ppermute | solution.py:45
  16.0 15.4 %collective-permute-start.6 = (bf16[352,768]{1,0:T(8,128)(2,1)S(1)}, bf16[352,768]{1,0:T(8,128)(2,1)S(1)}, u32[]{:S(2)}, u32[]{:S(2)}) collective-permute-start(bf16[352,768]{1,0:T(8,128)(2,1)S(1)} %pad_maximum_fusion.1), channel_id=1, source_target_pairs={{0,48},{8,200},{16,0},{24,216},{32,16},{40,232},{48,32},{56,248},{... | collective-permute-start | bytes 1622024 | tf_op jit(solution)/shard_map/ppermute | solution.py:26
  23.0 7.8 %collective-permute-start.5 = (bf16[256,768]{1,0:T(8,128)(2,1)S(1)}, bf16[256,768]{1,0:T(8,128)(2,1)S(1)}, u32[]{:S(2)}, u32[]{:S(2)}) collective-permute-start(bf16[256,768]{1,0:T(8,128)(2,1)S(1)} %constant_dynamic-update-slice_fusion), channel_id=1, source_target_pairs={{0,8},{8,0},{1,9},{9,1},{2,10},{10,2},{3,11},{11,3},{4,12},{12,4},... | collective-permute-start | bytes 1179656 | tf_op jit(solution)/shard_map/ppermute | solution.py:40
  24.9 9.9 %collective-permute-start.7 = (bf16[352,768]{1,0:T(8,128)(2,1)S(1)}, bf16[352,768]{1,0:T(8,128)(2,1)S(1)}, u32[]{:S(2)}, u32[]{:S(2)}) collective-permute-start(bf16[352,768]{1,0:T(8,128)(2,1)S(1)} %pad_maximum_fusion.2), channel_id=1, source_target_pairs={{0,16},{8,72},{16,32},{24,88},{32,48},{40,104},{48,0},{56,120},{64... | collective-permute-start | bytes 1622024 | tf_op jit(solution)/shard_map/ppermute | solution.py:26
  26.3 21.4 %collective-permute-start.8 = (bf16[352,768]{1,0:T(8,128)(2,1)S(1)}, bf16[352,768]{1,0:T(8,128)(2,1)S(1)}, u32[]{:S(2)}, u32[]{:S(2)}) collective-permute-start(bf16[352,768]{1,0:T(8,128)(2,1)S(1)} %pad_maximum_fusion.3), channel_id=1, source_target_pairs={{0,32},{8,136},{16,48},{24,152},{32,0},{40,168},{48,16},{56,184},{... | collective-permute-start | bytes 1622024 | tf_op jit(solution)/shard_map/ppermute | solution.py:26
  35.5 17.0 %collective-permute-start.9 = (bf16[512,768]{1,0:T(8,128)(2,1)S(1)}, bf16[512,768]{1,0:T(8,128)(2,1)S(1)}, u32[]{:S(2)}, u32[]{:S(2)}) collective-permute-start(bf16[512,768]{1,0:T(8,128)(2,1)S(1)} %convolution_convert_fusion.2), channel_id=1, source_target_pairs={{0,32},{8,136},{16,48},{24,152},{32,0},{40,168},{48,16},{56,184},{... | collective-permute-start | bytes 2359304 | tf_op jit(solution)/shard_map/ppermute | solution.py:26
  43.8 17.0 %collective-permute-start.10 = (bf16[512,768]{1,0:T(8,128)(2,1)S(1)}, bf16[512,768]{1,0:T(8,128)(2,1)S(1)}, u32[]{:S(2)}, u32[]{:S(2)}) collective-permute-start(bf16[512,768]{1,0:T(8,128)(2,1)S(1)} %convolution_convert_fusion.1), channel_id=1, source_target_pairs={{0,16},{8,72},{16,32},{24,88},{32,48},{40,104},{48,0},{56,120},{64... | collective-permute-start | bytes 2359304 | tf_op jit(solution)/shard_map/ppermute | solution.py:26
  44.7 16.1 %collective-permute-start.11 = (bf16[512,768]{1,0:T(8,128)(2,1)S(1)}, bf16[512,768]{1,0:T(8,128)(2,1)S(1)}, u32[]{:S(2)}, u32[]{:S(2)}) collective-permute-start(bf16[512,768]{1,0:T(8,128)(2,1)S(1)} %convolution_convert_fusion), channel_id=1, source_target_pairs={{0,48},{8,200},{16,0},{24,216},{32,16},{40,232},{48,32},{56,248},{... | collective-permute-start | bytes 2359304 | tf_op jit(solution)/shard_map/ppermute | solution.py:26
  61.2 7.0 %collective-permute-start.12 = (bf16[256,768]{1,0:T(8,128)(2,1)S(1)}, bf16[256,768]{1,0:T(8,128)(2,1)S(1)}, u32[]{:S(2)}, u32[]{:S(2)}) collective-permute-start(bf16[256,768]{1,0:T(8,128)(2,1)S(1)} %get-tuple-element.31), channel_id=1, source_target_pairs={{0,64},{8,24},{16,80},{24,8},{32,96},{40,56},{48,112},{56,40},{64,... | collective-permute-start | bytes 1179656 | tf_op jit(solution)/shard_map/ppermute | solution.py:36
  62.2 8.1 %collective-permute-start.14 = (bf16[256,768]{1,0:T(8,128)(2,1)S(1)}, bf16[256,768]{1,0:T(8,128)(2,1)S(1)}, u32[]{:S(2)}, u32[]{:S(2)}) collective-permute-start(bf16[256,768]{1,0:T(8,128)(2,1)S(1)} %get-tuple-element.32), channel_id=1, source_target_pairs={{0,192},{8,56},{16,208},{24,40},{32,224},{40,24},{48,240},{56,8},{... | collective-permute-start | bytes 1179656 | tf_op jit(solution)/shard_map/ppermute | solution.py:36
  70.6 8.2 %collective-permute-start.13 = (bf16[256,768]{1,0:T(8,128)(2,1)S(1)}, bf16[256,768]{1,0:T(8,128)(2,1)S(1)}, u32[]{:S(2)}, u32[]{:S(2)}) collective-permute-start(bf16[256,768]{1,0:T(8,128)(2,1)S(1)} %get-tuple-element.29), channel_id=1, source_target_pairs={{0,192},{8,56},{16,208},{24,40},{32,224},{40,24},{48,240},{56,8},{... | collective-permute-start | bytes 1179656 | tf_op jit(solution)/shard_map/ppermute | solution.py:36
  72.8 6.9 %collective-permute-start.15 = (bf16[256,768]{1,0:T(8,128)(2,1)S(1)}, bf16[256,768]{1,0:T(8,128)(2,1)S(1)}, u32[]{:S(2)}, u32[]{:S(2)}) collective-permute-start(bf16[256,768]{1,0:T(8,128)(2,1)S(1)} %get-tuple-element.30), channel_id=1, source_target_pairs={{0,64},{8,24},{16,80},{24,8},{32,96},{40,56},{48,112},{56,40},{64,... | collective-permute-start | bytes 1179656 | tf_op jit(solution)/shard_map/ppermute | solution.py:36
  80.5 8.2 %collective-permute-start.16 = (bf16[352,512]{1,0:T(8,128)(2,1)S(1)}, bf16[352,512]{1,0:T(8,128)(2,1)S(1)}, u32[]{:S(2)}, u32[]{:S(2)}) collective-permute-start(bf16[352,512]{1,0:T(8,128)(2,1)S(1)} %convolution_convert_fusion.5), channel_id=1, source_target_pairs={{0,32},{8,136},{16,48},{24,152},{32,0},{40,168},{48,16},{56,184},{... | collective-permute-start | bytes 1081352 | tf_op jit(solution)/shard_map/ppermute | solution.py:26
  82.8 9.7 %collective-permute-start.17 = (bf16[352,512]{1,0:T(8,128)(2,1)S(1)}, bf16[352,512]{1,0:T(8,128)(2,1)S(1)}, u32[]{:S(2)}, u32[]{:S(2)}) collective-permute-start(bf16[352,512]{1,0:T(8,128)(2,1)S(1)} %convolution_convert_fusion.4), channel_id=1, source_target_pairs={{0,16},{8,72},{16,32},{24,88},{32,48},{40,104},{48,0},{56,120},{64... | collective-permute-start | bytes 1081352 | tf_op jit(solution)/shard_map/ppermute | solution.py:26
  83.4 9.1 %collective-permute-start.18 = (bf16[352,512]{1,0:T(8,128)(2,1)S(1)}, bf16[352,512]{1,0:T(8,128)(2,1)S(1)}, u32[]{:S(2)}, u32[]{:S(2)}) collective-permute-start(bf16[352,512]{1,0:T(8,128)(2,1)S(1)} %convolution_convert_fusion.3), channel_id=1, source_target_pairs={{0,48},{8,200},{16,0},{24,216},{32,16},{40,232},{48,32},{56,248},{... | collective-permute-start | bytes 1081352 | tf_op jit(solution)/shard_map/ppermute | solution.py:26
  92.7 3.8 %collective-permute-start.19 = (f32[176,512]{1,0:T(8,128)S(1)}, f32[176,512]{1,0:T(8,128)S(1)}, u32[]{:S(2)}, u32[]{:S(2)}) collective-permute-start(f32[176,512]{1,0:T(8,128)S(1)} %slice.57), channel_id=1, source_target_pairs={{0,8},{8,0},{1,9},{9,1},{2,10},{10,2},{3,11},{11,3},{4,12},{12,4},... | collective-permute-start | bytes 1081352 | tf_op jit(solution)/shard_map/ppermute | solution.py:40

commit v3 on v2

--- a/solution.py
+++ b/solution.py
@@ -47,18 +47,19 @@
 
 def pick_columns(slots, screen, coef, width, first, second):
     rows = coef.shape[0]
-    count = slots.shape[0] // (N * N * C)
+    every = slots.shape[0]
+    count = every // (N * N * C)
     tile = 2 * width
 
-    def kernel(place_ref, slots_ref, screen_ref, coef_ref, out):
+    def kernel(place_ref, table_ref, coef_ref, out):
         lane = lax.broadcasted_iota(jnp.int32, (rows, tile), 1)
         for p in range(count):
             halves = []
             for side in range(2):
                 run, s = divmod(2 * p + side, count)
-                block = slots_ref[place_ref[run] * count + s]
+                block = table_ref[place_ref[run] * count + s]
                 at = pl.multiple_of(block // 2 * tile, tile)
-                value = coef_ref[:, pl.ds(at, tile)].astype(F32) * screen_ref[block].astype(F32)
+                value = coef_ref[:, pl.ds(at, tile)].astype(F32) * table_ref[every + block].astype(F32)
                 halves.append(jnp.where(block % 2 != side, pltpu.roll(value, width, 1), value))
             out[:, p * tile : (p + 1) * tile] = jnp.where(lane < width, halves[0], halves[1]).astype(BF16)
 
@@ -66,11 +67,11 @@
     return pl.pallas_call(
         kernel,
         out_shape=jax.ShapeDtypeStruct((rows, 2 * count * width), BF16),
-        in_specs=[smem, smem, smem, vmem],
+        in_specs=[smem, smem, vmem],
         out_specs=vmem,
         compiler_params=pltpu.CompilerParams(vmem_limit_bytes=20 << 20),
         name="pick",
-    )(jnp.stack([first, second]).astype(jnp.int32), slots, screen, coef)
+    )(jnp.stack([first, second]).astype(jnp.int32), jnp.concatenate([slots, screen]), coef)
 
 
 def turned(parts, places, height):
@@ -80,17 +81,17 @@
     return lax.dynamic_slice_in_dim(jnp.concatenate([whole, whole], axis=0), start, rows, 0)
 
 
-def gather_layers(own, core, z, *ready):
+def gather_layers(own, near, core, z, before):
     rows, cols = own.shape
-    next_one = layers(own, 1)
-    next_two = layers(own, 2)
-    pair = layers(after(jnp.concatenate([next_one, next_two], axis=0), *ready), 2)
+    next_one, next_two = near
+    sent, *before = lax.optimization_barrier((jnp.concatenate([next_one, next_two], axis=0), *before))
+    pair = layers(sent, 2)
     got = jnp.concatenate([next_one, next_two, pair], axis=0)
     other = swap(got)
     other = jnp.concatenate([other[:, cols // 2 :], other[:, : cols // 2]], axis=1)
     up, down = jnp.where(core == 0, got, other), jnp.where(core == 0, other, got)
     up, down = up.reshape(4, rows, cols), down.reshape(4, rows, cols)
-    return turned([down[0], own, up[0], up[1], up[2], up[3], down[2], down[1]], 1 - z, rows)
+    return turned([down[0], own, up[0], up[1], up[2], up[3], down[2], down[1]], 1 - z, rows), before
 
 
 def block_of(value, index, width, axis):
@@ -122,19 +123,19 @@
         at = N * core + (first - step) % N
         return jnp.concatenate([block_of(mo_virtual, at, width, 1), block_of(virt_taken, at, width, 1)], axis=0)
 
+    near = [layers(own, 1), layers(own, 2)]
     virt = [virt_block(0)] + [hop(virt_block(s), 0, N - s) for s in (1, 2, 3)]
-    chosen = gather_layers(own, core, z, ints_taken)
-    chosen = after(chosen, virt[1], virt[3])
+    chosen, ints = gather_layers(own, near, core, z, (half_ints, ints_taken))
 
     def product(step, chosen):
-        both = jnp.concatenate([ints_block(half_ints, step), ints_block(ints_taken, step)], axis=0)
+        both = jnp.concatenate([ints_block(a, step) for a in ints], axis=0)
         return jnp.dot(chosen, both, preferred_element_type=F32)
 
     got = [hop(product(s, chosen).astype(BF16), 0, s) for s in ORDER]
-    kept = lax.optimization_barrier(product(0, after(chosen, virt[2])))
+    kept = lax.optimization_barrier(product(0, after(chosen, *virt[1:])))
     total = add([kept, *got])
-    half = total.shape[0] // 2
-    ends = [total[:half], total[half:]]
+    rows = total.shape[0] // 2
+    ends = [total[:rows], total[rows:]]
     for masks in ((1, 3), (3, 1)):
         ends = [part + exchange(part.astype(BF16), 1, mask).astype(F32) for part, mask in zip(ends, masks)]
     ends = [part.astype(BF16) for part in ends]

time: 97.4 us -> 95.8 us (0.984)
  starting transfers between devices: 38 us -> 33.7 us
  waiting for transfers between devices: 43.5 us -> 47.3 us
  local copies, waits for them, and re-layouts: 7.39 us -> 5.1 us
    ppermute x9, starting transfers between devices: 22.1 us -> 16.1 us  [hop(): return lax.ppermute(value, PAIR, pairs)]
    ppermute x9, waiting for transfers between devices: 21.7 us -> 24.2 us  [hop(): return lax.ppermute(value, PAIR, pairs)]
    ppermute x4, starting transfers between devices: 7.54 us -> 9.59 us  [swap(): return lax.ppermute(value, 'core', [(0, 1), (1, 0)])]
    unnamed x17 -> x13, local copies, waits for them, and re-layouts: 3.26 us -> 1.49 us
    ppermute x3, waiting for transfers between devices: 7.56 us -> 8.55 us  [layers(): return lax.ppermute(value, ('core', 'z'), pairs)]
    dynamic_slice x4 -> x3, local copies, waits for them, and re-layouts: 3.9 us -> 3.39 us  [block_of(): return lax.dynamic_slice_in_dim(value, index * width, width, axis)]
  transfers between devices with their start and end apart: 20 -> 20, of which waited for: 13 -> 13; matrix products, arithmetic and copies ran while one was open for 9% -> 10% of each run, Pallas kernels for 1% -> 1%
where the time goes in v3:
time: 95.8 us; the launch traced here: 95.2 us
  waiting for transfers between devices  47.3 us (49%)
  starting transfers between devices  33.7 us (35%)
  local copies, waits for them, and re-layouts  5.1 us (5%)
  matrix products  5.04 us (5%)
  other arithmetic  3.01 us (3%)
    ppermute x9, waiting for transfers between devices, hop(): return lax.ppermute(value, PAIR, pairs)  24.2 us
    ppermute x9, starting transfers between devices, hop(): return lax.ppermute(value, PAIR, pairs)  16.1 us
    ppermute x4, waiting for transfers between devices, exchange(): return lax.ppermute(value, PAIR, pairs)  13.2 us
    ppermute x4, starting transfers between devices, swap(): return lax.ppermute(value, 'core', [(0, 1), (1, 0)])  9.59 us
    ppermute x3, waiting for transfers between devices, layers(): return lax.ppermute(value, ('core', 'z'), pairs)  8.55 us
    ppermute x4, starting transfers between devices, exchange(): return lax.ppermute(value, PAIR, pairs)  4.72 us
    dynamic_slice x3, local copies, waits for them, and re-layouts, block_of(): return lax.dynamic_slice_in_dim(value, index * width, width, axis)  3.39 us
    ppermute x3, starting transfers between devices, layers(): return lax.ppermute(value, ('core', 'z'), pairs)  3.32 us
  transfers between devices with their start and end apart: 20, of which 13 were waited for; matrix products, arithmetic and copies ran while one was open for 10% of the time, Pallas kernels for 1%

profile of v3, /device:TPU:1, one launch (start us, length us, event | category | flops | bytes accessed | tf_op | source)
XLA Modules:
  0.0 95.2 jit_solution(503634156254007400)
XLA Ops:
  0.0 3.2 %collective-permute-start.3 = (bf16[1,384,6144]{2,1,0:T(8,128)(2,1)}, bf16[1,384,6144]{2,1,0:T(8,128)(2,1)}, u32[]{:S(2)}, u32[]{:S(2)}) collective-permute-start(bf16[1,384,6144]{2,1,0:T(8,128)(2,1)} %param.5), channel_id=1, source_target_pairs={{0,8},{8,0},{1,9},{9,1},{2,10},{10,2},{3,11},{11,3},{4,12},{12,4},... | collective-permute-start | bytes 14155784 | tf_op jit(solution)/shard_map/ppermute | solution.py:40
  4.1 1.4 %copy-done = bf16[64,12288]{1,0:T(8,128)(2,1)S(1)} copy-done((bf16[64,12288]{1,0:T(8,128)(2,1)S(1)}, bf16[64,12288]{1,0:T(8,128)(2,1)}, u32[]{:S(2)}) %copy-start) | copy-done | bytes 1572888
  6.3 2.9 %collective-permute-start.2 = (bf16[64,768]{1,0:T(8,128)(2,1)S(1)}, bf16[64,768]{1,0:T(8,128)(2,1)S(1)}, u32[]{:S(2)}, u32[]{:S(2)}) collective-permute-start(bf16[64,768]{1,0:T(8,128)(2,1)S(1)} %pick.1), channel_id=1, source_target_pairs={{0,6},{1,7},{2,0},{3,1},{4,2},{5,3},{6,4},{7,5},{8,10},{9,11},{10,... | collective-permute-start | bytes 294920 | tf_op jit(solution)/shard_map/ppermute | solution.py:45
  9.2 1.3 %constant_dynamic-slice_fusion.8 = (bf16[176,768]{1,0:T(8,128)(2,1)S(1)}, bf16[176,768]{1,0:T(8,128)(2,1)S(1)}, bf16[176,768]{1,0:T(8,128)(2,1)S(1)}, bf16[176,768]{1,0:T(8,128)(2,1)S(1)}) fusion(bf16[176,6144]{1,0:T(8,128)(2,1)} %param.7, s32[]{:T(128)S(6)} %select_n.95, s32[]{:T(128)S(6)} %select_n.102, s32[]{:T(128)S(6)} %select_n.106, s32[]{:T(128)S(6)} %select_n.104), kind=kLoop, calls=%fused_computation.73 | loop fusion | bytes 2162704 | tf_op jit(solution)/shard_map/dynamic_slice | solution.py:98
  10.5 1.7 %collective-permute-done.1 = bf16[64,768]{1,0:T(8,128)(2,1)S(1)} collective-permute-done((bf16[64,768]{1,0:T(8,128)(2,1)S(1)}, bf16[64,768]{1,0:T(8,128)(2,1)S(1)}, u32[]{:S(2)}, u32[]{:S(2)}) %collective-permute-start.1) | collective-permute-done | bytes 98336 | tf_op jit(solution)/shard_map/ppermute | solution.py:45
  12.2 2.9 %collective-permute-done.2 = bf16[64,768]{1,0:T(8,128)(2,1)S(1)} collective-permute-done((bf16[64,768]{1,0:T(8,128)(2,1)S(1)}, bf16[64,768]{1,0:T(8,128)(2,1)S(1)}, u32[]{:S(2)}, u32[]{:S(2)}) %collective-permute-start.2) | collective-permute-done | bytes 98336 | tf_op jit(solution)/shard_map/ppermute | solution.py:45
  15.6 2.8 %collective-permute-start.6 = (bf16[352,768]{1,0:T(8,128)(2,1)S(1)}, bf16[352,768]{1,0:T(8,128)(2,1)S(1)}, u32[]{:S(2)}, u32[]{:S(2)}) collective-permute-start(bf16[352,768]{1,0:T(8,128)(2,1)S(1)} %pad_maximum_fusion.1), channel_id=1, source_target_pairs={{0,48},{8,200},{16,0},{24,216},{32,16},{40,232},{48,32},{56,248},{... | collective-permute-start | bytes 1622024 | tf_op jit(solution)/shard_map/ppermute | solution.py:26
  18.4 4.0 %collective-permute-done.4 = bf16[128,768]{1,0:T(8,128)(2,1)S(1)} collective-permute-done((bf16[128,768]{1,0:T(8,128)(2,1)S(1)}, bf16[128,768]{1,0:T(8,128)(2,1)S(1)}, u32[]{:S(2)}, u32[]{:S(2)}) %collective-permute-start.4) | collective-permute-done | bytes 196640 | tf_op jit(solution)/shard_map/ppermute | solution.py:45
  22.4 1.8 %collective-permute-start.5 = (bf16[256,768]{1,0:T(8,128)(2,1)S(1)}, bf16[256,768]{1,0:T(8,128)(2,1)S(1)}, u32[]{:S(2)}, u32[]{:S(2)}) collective-permute-start(bf16[256,768]{1,0:T(8,128)(2,1)S(1)} %constant_dynamic-update-slice_fusion), channel_id=1, source_target_pairs={{0,8},{8,0},{1,9},{9,1},{2,10},{10,2},{3,11},{11,3},{4,12},{12,4},... | collective-permute-start | bytes 1179656 | tf_op jit(solution)/shard_map/ppermute | solution.py:40
  24.3 3.0 %collective-permute-start.7 = (bf16[352,768]{1,0:T(8,128)(2,1)S(1)}, bf16[352,768]{1,0:T(8,128)(2,1)S(1)}, u32[]{:S(2)}, u32[]{:S(2)}) collective-permute-start(bf16[352,768]{1,0:T(8,128)(2,1)S(1)} %pad_maximum_fusion.2), channel_id=1, source_target_pairs={{0,32},{8,136},{16,48},{24,152},{32,0},{40,168},{48,16},{56,184},{... | collective-permute-start | bytes 1622024 | tf_op jit(solution)/shard_map/ppermute | solution.py:26
  27.8 2.0 %dynamic-slice_bitcast_fusion.4 = (bf16[384,768]{1,0:T(8,128)(2,1)S(1)}, bf16[384,768]{1,0:T(8,128)(2,1)S(1)}, bf16[384,768]{1,0:T(8,128)(2,1)S(1)}, bf16[384,76...) fusion(bf16[1,384,6144]{2,1,0:T(8,128)(2,1)} %collective-permut, ...), kind=kLoop, calls=%fused_computation.32 | loop fusion | bytes 9437200 | tf_op jit(solution)/shard_map/dynamic_slice | solution.py:98
  30.4 0.8 convolution_convert_fusion.2
  31.2 1.6 %collective-permute-start.9 = (bf16[512,768]{1,0:T(8,128)(2,1)S(1)}, bf16[512,768]{1,0:T(8,128)(2,1)S(1)}, u32[]{:S(2)}, u32[]{:S(2)}) collective-permute-start(bf16[512,768]{1,0:T(8,128)(2,1)S(1)} %convolution_convert_fusion.2), channel_id=1, source_target_pairs={{0,32},{8,136},{16,48},{24,152},{32,0},{40,168},{48,16},{56,184},{... | collective-permute-start | bytes 2359304 | tf_op jit(solution)/shard_map/ppermute | solution.py:26
  32.8 0.8 convolution_convert_fusion.1
  33.6 1.4 %collective-permute-start.10 = (bf16[512,768]{1,0:T(8,128)(2,1)S(1)}, bf16[512,768]{1,0:T(8,128)(2,1)S(1)}, u32[]{:S(2)}, u32[]{:S(2)}) collective-permute-start(bf16[512,768]{1,0:T(8,128)(2,1)S(1)} %convolution_convert_fusion.1), channel_id=1, source_target_pairs={{0,16},{8,72},{16,32},{24,88},{32,48},{40,104},{48,0},{56,120},{64... | collective-permute-start | bytes 2359304 | tf_op jit(solution)/shard_map/ppermute | solution.py:26
  35.0 0.8 convolution_convert_fusion
  35.8 1.6 %collective-permute-start.11 = (bf16[512,768]{1,0:T(8,128)(2,1)S(1)}, bf16[512,768]{1,0:T(8,128)(2,1)S(1)}, u32[]{:S(2)}, u32[]{:S(2)}) collective-permute-start(bf16[512,768]{1,0:T(8,128)(2,1)S(1)} %convolution_convert_fusion), channel_id=1, source_target_pairs={{0,48},{8,200},{16,0},{24,216},{32,16},{40,232},{48,32},{56,248},{... | collective-permute-start | bytes 2359304 | tf_op jit(solution)/shard_map/ppermute | solution.py:26
  37.4 2.7 %collective-permute-done.8 = bf16[352,768]{1,0:T(8,128)(2,1)S(1)} collective-permute-done((bf16[352,768]{1,0:T(8,128)(2,1)S(1)}, bf16[352,768]{1,0:T(8,128)(2,1)S(1)}, u32[]{:S(2)}, u32[]{:S(2)}) %collective-permute-start.8) | collective-permute-done | bytes 540704 | tf_op jit(solution)/shard_map/ppermute | solution.py:26
  40.9 7.7 %collective-permute-done.9 = bf16[512,768]{1,0:T(8,128)(2,1)S(1)} collective-permute-done((bf16[512,768]{1,0:T(8,128)(2,1)S(1)}, bf16[512,768]{1,0:T(8,128)(2,1)S(1)}, u32[]{:S(2)}, u32[]{:S(2)}) %collective-permute-start.9) | collective-permute-done | bytes 786464 | tf_op jit(solution)/shard_map/ppermute | solution.py:26
  48.7 8.3 %collective-permute-done.10 = bf16[512,768]{1,0:T(8,128)(2,1)S(1)} collective-permute-done((bf16[512,768]{1,0:T(8,128)(2,1)S(1)}, bf16[512,768]{1,0:T(8,128)(2,1)S(1)}, u32[]{:S(2)}, u32[]{:S(2)}) %collective-permute-start.10) | collective-permute-done | bytes 786464 | tf_op jit(solution)/shard_map/ppermute | solution.py:26
  57.4 1.0 %collective-permute-start.12 = (bf16[256,768]{1,0:T(8,128)(2,1)S(1)}, bf16[256,768]{1,0:T(8,128)(2,1)S(1)}, u32[]{:S(2)}, u32[]{:S(2)}) collective-permute-start(bf16[256,768]{1,0:T(8,128)(2,1)S(1)} %get-tuple-element.33), channel_id=1, source_target_pairs={{0,64},{8,24},{16,80},{24,8},{32,96},{40,56},{48,112},{56,40},{64,... | collective-permute-start | bytes 1179656 | tf_op jit(solution)/shard_map/ppermute | solution.py:36
  58.4 1.8 %collective-permute-start.14 = (bf16[256,768]{1,0:T(8,128)(2,1)S(1)}, bf16[256,768]{1,0:T(8,128)(2,1)S(1)}, u32[]{:S(2)}, u32[]{:S(2)}) collective-permute-start(bf16[256,768]{1,0:T(8,128)(2,1)S(1)} %get-tuple-element.34), channel_id=1, source_target_pairs={{0,192},{8,56},{16,208},{24,40},{32,224},{40,24},{48,240},{56,8},{... | collective-permute-start | bytes 1179656 | tf_op jit(solution)/shard_map/ppermute | solution.py:36
  60.2 4.2 %collective-permute-done.12 = bf16[256,768]{1,0:T(8,128)(2,1)S(1)} collective-permute-done((bf16[256,768]{1,0:T(8,128)(2,1)S(1)}, bf16[256,768]{1,0:T(8,128)(2,1)S(1)}, u32[]{:S(2)}, u32[]{:S(2)}) %collective-permute-start.12) | collective-permute-done | bytes 393248 | tf_op jit(solution)/shard_map/ppermute | solution.py:36
  64.4 2.1 %collective-permute-done.14 = bf16[256,768]{1,0:T(8,128)(2,1)S(1)} collective-permute-done((bf16[256,768]{1,0:T(8,128)(2,1)S(1)}, bf16[256,768]{1,0:T(8,128)(2,1)S(1)}, u32[]{:S(2)}, u32[]{:S(2)}) %collective-permute-start.14) | collective-permute-done | bytes 393248 | tf_op jit(solution)/shard_map/ppermute | solution.py:36
  66.8 1.9 %collective-permute-start.13 = (bf16[256,768]{1,0:T(8,128)(2,1)S(1)}, bf16[256,768]{1,0:T(8,128)(2,1)S(1)}, u32[]{:S(2)}, u32[]{:S(2)}) collective-permute-start(bf16[256,768]{1,0:T(8,128)(2,1)S(1)} %get-tuple-element.31), channel_id=1, source_target_pairs={{0,192},{8,56},{16,208},{24,40},{32,224},{40,24},{48,240},{56,8},{... | collective-permute-start | bytes 1179656 | tf_op jit(solution)/shard_map/ppermute | solution.py:36
  68.7 6.3 %collective-permute-done.13 = bf16[256,768]{1,0:T(8,128)(2,1)S(1)} collective-permute-done((bf16[256,768]{1,0:T(8,128)(2,1)S(1)}, bf16[256,768]{1,0:T(8,128)(2,1)S(1)}, u32[]{:S(2)}, u32[]{:S(2)}) %collective-permute-start.13) | collective-permute-done | bytes 393248 | tf_op jit(solution)/shard_map/ppermute | solution.py:36
  76.4 2.3 %collective-permute-start.16 = (bf16[352,512]{1,0:T(8,128)(2,1)S(1)}, bf16[352,512]{1,0:T(8,128)(2,1)S(1)}, u32[]{:S(2)}, u32[]{:S(2)}) collective-permute-start(bf16[352,512]{1,0:T(8,128)(2,1)S(1)} %convolution_convert_fusion.5), channel_id=1, source_target_pairs={{0,32},{8,136},{16,48},{24,152},{32,0},{40,168},{48,16},{56,184},{... | collective-permute-start | bytes 1081352 | tf_op jit(solution)/shard_map/ppermute | solution.py:26
  79.8 2.7 %collective-permute-start.18 = (bf16[352,512]{1,0:T(8,128)(2,1)S(1)}, bf16[352,512]{1,0:T(8,128)(2,1)S(1)}, u32[]{:S(2)}, u32[]{:S(2)}) collective-permute-start(bf16[352,512]{1,0:T(8,128)(2,1)S(1)} %convolution_convert_fusion.3), channel_id=1, source_target_pairs={{0,48},{8,200},{16,0},{24,216},{32,16},{40,232},{48,32},{56,248},{... | collective-permute-start | bytes 1081352 | tf_op jit(solution)/shard_map/ppermute | solution.py:26
  83.0 1.4 %collective-permute-done.16 = bf16[352,512]{1,0:T(8,128)(2,1)S(1)} collective-permute-done((bf16[352,512]{1,0:T(8,128)(2,1)S(1)}, bf16[352,512]{1,0:T(8,128)(2,1)S(1)}, u32[]{:S(2)}, u32[]{:S(2)}) %collective-permute-start.16) | collective-permute-done | bytes 360480 | tf_op jit(solution)/shard_map/ppermute | solution.py:26
  84.3 4.1 %collective-permute-done.17 = bf16[352,512]{1,0:T(8,128)(2,1)S(1)} collective-permute-done((bf16[352,512]{1,0:T(8,128)(2,1)S(1)}, bf16[352,512]{1,0:T(8,128)(2,1)S(1)}, u32[]{:S(2)}, u32[]{:S(2)}) %collective-permute-start.17) | collective-permute-done | bytes 360480 | tf_op jit(solution)/shard_map/ppermute | solution.py:26
  88.6 4.5 %collective-permute-start.19 = (f32[176,512]{1,0:T(8,128)S(1)}, f32[176,512]{1,0:T(8,128)S(1)}, u32[]{:S(2)}, u32[]{:S(2)}) collective-permute-start(f32[176,512]{1,0:T(8,128)S(1)} %slice.57), channel_id=1, source_target_pairs={{0,8},{8,0},{1,9},{9,1},{2,10},{10,2},{3,11},{11,3},{4,12},{12,4},... | collective-permute-start | bytes 1081352 | tf_op jit(solution)/shard_map/ppermute | solution.py:40
  93.2 1.3 %collective-permute-done.19 = f32[176,512]{1,0:T(8,128)S(1)} collective-permute-done((f32[176,512]{1,0:T(8,128)S(1)}, f32[176,512]{1,0:T(8,128)S(1)}, u32[]{:S(2)}, u32[]{:S(2)}) %collective-permute-start.19) | collective-permute-done | bytes 360480 | tf_op jit(solution)/shard_map/ppermute | solution.py:40
  (53 shorter events, 8.5 us)
Async XLA Ops:
  0.0 15.1 %collective-permute-start.3 = (bf16[1,384,6144]{2,1,0:T(8,128)(2,1)}, bf16[1,384,6144]{2,1,0:T(8,128)(2,1)}, u32[]{:S(2)}, u32[]{:S(2)}) collective-permute-start(bf16[1,384,6144]{2,1,0:T(8,128)(2,1)} %param.5), channel_id=1, source_target_pairs={{0,8},{8,0},{1,9},{9,1},{2,10},{10,2},{3,11},{11,3},{4,12},{12,4},... | collective-permute-start | bytes 14155784 | tf_op jit(solution)/shard_map/ppermute | solution.py:40
  3.2 12.2 %collective-permute-start = (bf16[176,6144]{1,0:T(8,128)(2,1)}, bf16[176,6144]{1,0:T(8,128)(2,1)S(1)}, u32[]{:S(2)}, u32[]{:S(2)}) collective-permute-start(bf16[176,6144]{1,0:T(8,128)(2,1)} %param.7), channel_id=1, source_target_pairs={{0,8},{8,0},{1,9},{9,1},{2,10},{10,2},{3,11},{11,3},{4,12},{12,4},... | collective-permute-start | bytes 6488072 | tf_op jit(solution)/shard_map/ppermute | solution.py:40
  4.1 1.4 %copy-start = (bf16[64,12288]{1,0:T(8,128)(2,1)S(1)}, bf16[64,12288]{1,0:T(8,128)(2,1)}, u32[]{:S(2)}) copy-start(bf16[64,12288]{1,0:T(8,128)(2,1)} %coef_ref.1) | copy-start | bytes 4718596
  6.2 5.9 %collective-permute-start.1 = (bf16[64,768]{1,0:T(8,128)(2,1)S(1)}, bf16[64,768]{1,0:T(8,128)(2,1)S(1)}, u32[]{:S(2)}, u32[]{:S(2)}) collective-permute-start(bf16[64,768]{1,0:T(8,128)(2,1)S(1)} %pick.1), channel_id=1, source_target_pairs={{0,7},{1,0},{2,1},{3,2},{4,3},{5,4},{6,5},{7,6},{8,9},{9,10},{10,1... | collective-permute-start | bytes 294920 | tf_op jit(solution)/shard_map/ppermute | solution.py:45
  6.3 8.7 %collective-permute-start.2 = (bf16[64,768]{1,0:T(8,128)(2,1)S(1)}, bf16[64,768]{1,0:T(8,128)(2,1)S(1)}, u32[]{:S(2)}, u32[]{:S(2)}) collective-permute-start(bf16[64,768]{1,0:T(8,128)(2,1)S(1)} %pick.1), channel_id=1, source_target_pairs={{0,6},{1,7},{2,0},{3,1},{4,2},{5,3},{6,4},{7,5},{8,10},{9,11},{10,... | collective-permute-start | bytes 294920 | tf_op jit(solution)/shard_map/ppermute | solution.py:45
  15.1 7.3 %collective-permute-start.4 = (bf16[128,768]{1,0:T(8,128)(2,1)S(1)}, bf16[128,768]{1,0:T(8,128)(2,1)S(1)}, u32[]{:S(2)}, u32[]{:S(2)}) collective-permute-start(bf16[128,768]{1,0:T(8,128)(2,1)S(1)} %pad_maximum_fusion.5), channel_id=1, source_target_pairs={{0,6},{1,7},{2,0},{3,1},{4,2},{5,3},{6,4},{7,5},{8,10},{9,11},{10,... | collective-permute-start | bytes 589832 | tf_op jit(solution)/shard_map/ppermute | solution.py:45
  15.5 12.3 %copy-start.1 = (bf16[1,384,6144]{2,1,0:T(8,128)(2,1)S(1)}, bf16[1,384,6144]{2,1,0:T(8,128)(2,1)}, u32[]{:S(2)}) copy-start(bf16[1,384,6144]{2,1,0:T(8,128)(2,1)} %param.5) | copy-start | bytes 14155780
  15.6 20.2 %collective-permute-start.6 = (bf16[352,768]{1,0:T(8,128)(2,1)S(1)}, bf16[352,768]{1,0:T(8,128)(2,1)S(1)}, u32[]{:S(2)}, u32[]{:S(2)}) collective-permute-start(bf16[352,768]{1,0:T(8,128)(2,1)S(1)} %pad_maximum_fusion.1), channel_id=1, source_target_pairs={{0,48},{8,200},{16,0},{24,216},{32,16},{40,232},{48,32},{56,248},{... | collective-permute-start | bytes 1622024 | tf_op jit(solution)/shard_map/ppermute | solution.py:26
  22.4 7.4 %collective-permute-start.5 = (bf16[256,768]{1,0:T(8,128)(2,1)S(1)}, bf16[256,768]{1,0:T(8,128)(2,1)S(1)}, u32[]{:S(2)}, u32[]{:S(2)}) collective-permute-start(bf16[256,768]{1,0:T(8,128)(2,1)S(1)} %constant_dynamic-update-slice_fusion), channel_id=1, source_target_pairs={{0,8},{8,0},{1,9},{9,1},{2,10},{10,2},{3,11},{11,3},{4,12},{12,4},... | collective-permute-start | bytes 1179656 | tf_op jit(solution)/shard_map/ppermute | solution.py:40
  24.3 13.2 %collective-permute-start.7 = (bf16[352,768]{1,0:T(8,128)(2,1)S(1)}, bf16[352,768]{1,0:T(8,128)(2,1)S(1)}, u32[]{:S(2)}, u32[]{:S(2)}) collective-permute-start(bf16[352,768]{1,0:T(8,128)(2,1)S(1)} %pad_maximum_fusion.2), channel_id=1, source_target_pairs={{0,32},{8,136},{16,48},{24,152},{32,0},{40,168},{48,16},{56,184},{... | collective-permute-start | bytes 1622024 | tf_op jit(solution)/shard_map/ppermute | solution.py:26
  27.3 12.8 %collective-permute-start.8 = (bf16[352,768]{1,0:T(8,128)(2,1)S(1)}, bf16[352,768]{1,0:T(8,128)(2,1)S(1)}, u32[]{:S(2)}, u32[]{:S(2)}) collective-permute-start(bf16[352,768]{1,0:T(8,128)(2,1)S(1)} %pad_maximum_fusion.3), channel_id=1, source_target_pairs={{0,16},{8,72},{16,32},{24,88},{32,48},{40,104},{48,0},{56,120},{64... | collective-permute-start | bytes 1622024 | tf_op jit(solution)/shard_map/ppermute | solution.py:26
  31.2 17.5 %collective-permute-start.9 = (bf16[512,768]{1,0:T(8,128)(2,1)S(1)}, bf16[512,768]{1,0:T(8,128)(2,1)S(1)}, u32[]{:S(2)}, u32[]{:S(2)}) collective-permute-start(bf16[512,768]{1,0:T(8,128)(2,1)S(1)} %convolution_convert_fusion.2), channel_id=1, source_target_pairs={{0,32},{8,136},{16,48},{24,152},{32,0},{40,168},{48,16},{56,184},{... | collective-permute-start | bytes 2359304 | tf_op jit(solution)/shard_map/ppermute | solution.py:26
  33.6 23.4 %collective-permute-start.10 = (bf16[512,768]{1,0:T(8,128)(2,1)S(1)}, bf16[512,768]{1,0:T(8,128)(2,1)S(1)}, u32[]{:S(2)}, u32[]{:S(2)}) collective-permute-start(bf16[512,768]{1,0:T(8,128)(2,1)S(1)} %convolution_convert_fusion.1), channel_id=1, source_target_pairs={{0,16},{8,72},{16,32},{24,88},{32,48},{40,104},{48,0},{56,120},{64... | collective-permute-start | bytes 2359304 | tf_op jit(solution)/shard_map/ppermute | solution.py:26
  35.8 21.2 %collective-permute-start.11 = (bf16[512,768]{1,0:T(8,128)(2,1)S(1)}, bf16[512,768]{1,0:T(8,128)(2,1)S(1)}, u32[]{:S(2)}, u32[]{:S(2)}) collective-permute-start(bf16[512,768]{1,0:T(8,128)(2,1)S(1)} %convolution_convert_fusion), channel_id=1, source_target_pairs={{0,48},{8,200},{16,0},{24,216},{32,16},{40,232},{48,32},{56,248},{... | collective-permute-start | bytes 2359304 | tf_op jit(solution)/shard_map/ppermute | solution.py:26
  57.4 7.0 %collective-permute-start.12 = (bf16[256,768]{1,0:T(8,128)(2,1)S(1)}, bf16[256,768]{1,0:T(8,128)(2,1)S(1)}, u32[]{:S(2)}, u32[]{:S(2)}) collective-permute-start(bf16[256,768]{1,0:T(8,128)(2,1)S(1)} %get-tuple-element.33), channel_id=1, source_target_pairs={{0,64},{8,24},{16,80},{24,8},{32,96},{40,56},{48,112},{56,40},{64,... | collective-permute-start | bytes 1179656 | tf_op jit(solution)/shard_map/ppermute | solution.py:36
  58.4 8.1 %collective-permute-start.14 = (bf16[256,768]{1,0:T(8,128)(2,1)S(1)}, bf16[256,768]{1,0:T(8,128)(2,1)S(1)}, u32[]{:S(2)}, u32[]{:S(2)}) collective-permute-start(bf16[256,768]{1,0:T(8,128)(2,1)S(1)} %get-tuple-element.34), channel_id=1, source_target_pairs={{0,192},{8,56},{16,208},{24,40},{32,224},{40,24},{48,240},{56,8},{... | collective-permute-start | bytes 1179656 | tf_op jit(solution)/shard_map/ppermute | solution.py:36
  66.8 8.2 %collective-permute-start.13 = (bf16[256,768]{1,0:T(8,128)(2,1)S(1)}, bf16[256,768]{1,0:T(8,128)(2,1)S(1)}, u32[]{:S(2)}, u32[]{:S(2)}) collective-permute-start(bf16[256,768]{1,0:T(8,128)(2,1)S(1)} %get-tuple-element.31), channel_id=1, source_target_pairs={{0,192},{8,56},{16,208},{24,40},{32,224},{40,24},{48,240},{56,8},{... | collective-permute-start | bytes 1179656 | tf_op jit(solution)/shard_map/ppermute | solution.py:36
  68.7 6.9 %collective-permute-start.15 = (bf16[256,768]{1,0:T(8,128)(2,1)S(1)}, bf16[256,768]{1,0:T(8,128)(2,1)S(1)}, u32[]{:S(2)}, u32[]{:S(2)}) collective-permute-start(bf16[256,768]{1,0:T(8,128)(2,1)S(1)} %get-tuple-element.32), channel_id=1, source_target_pairs={{0,64},{8,24},{16,80},{24,8},{32,96},{40,56},{48,112},{56,40},{64,... | collective-permute-start | bytes 1179656 | tf_op jit(solution)/shard_map/ppermute | solution.py:36
  76.4 8.0 %collective-permute-start.16 = (bf16[352,512]{1,0:T(8,128)(2,1)S(1)}, bf16[352,512]{1,0:T(8,128)(2,1)S(1)}, u32[]{:S(2)}, u32[]{:S(2)}) collective-permute-start(bf16[352,512]{1,0:T(8,128)(2,1)S(1)} %convolution_convert_fusion.5), channel_id=1, source_target_pairs={{0,32},{8,136},{16,48},{24,152},{32,0},{40,168},{48,16},{56,184},{... | collective-permute-start | bytes 1081352 | tf_op jit(solution)/shard_map/ppermute | solution.py:26
  79.2 9.2 %collective-permute-start.17 = (bf16[352,512]{1,0:T(8,128)(2,1)S(1)}, bf16[352,512]{1,0:T(8,128)(2,1)S(1)}, u32[]{:S(2)}, u32[]{:S(2)}) collective-permute-start(bf16[352,512]{1,0:T(8,128)(2,1)S(1)} %convolution_convert_fusion.4), channel_id=1, source_target_pairs={{0,16},{8,72},{16,32},{24,88},{32,48},{40,104},{48,0},{56,120},{64... | collective-permute-start | bytes 1081352 | tf_op jit(solution)/shard_map/ppermute | solution.py:26
  79.8 8.6 %collective-permute-start.18 = (bf16[352,512]{1,0:T(8,128)(2,1)S(1)}, bf16[352,512]{1,0:T(8,128)(2,1)S(1)}, u32[]{:S(2)}, u32[]{:S(2)}) collective-permute-start(bf16[352,512]{1,0:T(8,128)(2,1)S(1)} %convolution_convert_fusion.3), channel_id=1, source_target_pairs={{0,48},{8,200},{16,0},{24,216},{32,16},{40,232},{48,32},{56,248},{... | collective-permute-start | bytes 1081352 | tf_op jit(solution)/shard_map/ppermute | solution.py:26
  88.6 5.8 %collective-permute-start.19 = (f32[176,512]{1,0:T(8,128)S(1)}, f32[176,512]{1,0:T(8,128)S(1)}, u32[]{:S(2)}, u32[]{:S(2)}) collective-permute-start(f32[176,512]{1,0:T(8,128)S(1)} %slice.57), channel_id=1, source_target_pairs={{0,8},{8,0},{1,9},{9,1},{2,10},{10,2},{3,11},{11,3},{4,12},{12,4},... | collective-permute-start | bytes 1081352 | tf_op jit(solution)/shard_map/ppermute | solution.py:40

commit v4 on v3

--- a/solution.py
+++ b/solution.py
@@ -141,13 +141,16 @@
     ends = [part.astype(BF16) for part in ends]
     summed = jnp.concatenate(ends, axis=0)
 
-    def fold(step):
-        return lax.dot_general(virt[step], summed, (((1,), (1,)), ((), ())), preferred_element_type=F32)
+    height = mo_virtual.shape[0]
 
-    got = [hop(fold(s).astype(BF16), 0, s) for s in ORDER]
-    both = add([lax.optimization_barrier(fold(0)), *got])
-    rows = mo_virtual.shape[0]
-    out = (both[:rows] + swap(both[rows:])).astype(BF16)
+    def fold(rows):
+        left = jnp.concatenate([virt[s][rows] for s in (*ORDER, 0)], axis=0)
+        return lax.dot_general(left, summed, (((1,), (1,)), ((), ())), preferred_element_type=F32)
+
+    whole = fold(slice(None))
+    parts = {s: block_of(whole, k, C * height, 0) for k, s in enumerate((*ORDER, 0))}
+    both = add([parts[0], *(hop(parts[s].astype(BF16), 0, s) for s in ORDER)])
+    out = (both[:height] + swap(both[height:])).astype(BF16)
     return out[:, None, :]
 
 

time: 95.8 us -> 97 us (1.013)
  waiting for transfers between devices: 47.3 us -> 51.2 us
  starting transfers between devices: 33.7 us -> 30.9 us
  local copies, waits for them, and re-layouts: 5.1 us -> 6.16 us
    ppermute x9, waiting for transfers between devices: 24.2 us -> 29.1 us  [hop(): return lax.ppermute(value, PAIR, pairs)]
    ppermute x9, starting transfers between devices: 16.1 us -> 13.6 us  [hop(): return lax.ppermute(value, PAIR, pairs)]
    ppermute x4, waiting for transfers between devices: 13.2 us -> 12.1 us  [exchange(): return lax.ppermute(value, PAIR, pairs)]
    unnamed x13 -> x17, local copies, waits for them, and re-layouts: 1.49 us -> 2.57 us
    dynamic_slice x3 -> x4, local copies, waits for them, and re-layouts: 3.39 us -> 3.32 us  [block_of(): return lax.dynamic_slice_in_dim(value, index * width, width, axis)]
  transfers between devices with their start and end apart: 20 -> 20, of which waited for: 13 -> 13; matrix products, arithmetic and copies ran while one was open for 10% -> 9% of each run, Pallas kernels for 1% -> 1%
where the time goes in v4:
time: 97 us; the launch traced here: 96.8 us
  waiting for transfers between devices  51.2 us (53%)
  starting transfers between devices  30.9 us (32%)
  local copies, waits for them, and re-layouts  6.16 us (6%)
  matrix products  4.46 us (5%)
  other arithmetic  3.01 us (3%)
    ppermute x9, waiting for transfers between devices, hop(): return lax.ppermute(value, PAIR, pairs)  29.1 us
    ppermute x9, starting transfers between devices, hop(): return lax.ppermute(value, PAIR, pairs)  13.6 us
    ppermute x4, waiting for transfers between devices, exchange(): return lax.ppermute(value, PAIR, pairs)  12.1 us
    ppermute x4, starting transfers between devices, swap(): return lax.ppermute(value, 'core', [(0, 1), (1, 0)])  9.33 us
    ppermute x3, waiting for transfers between devices, layers(): return lax.ppermute(value, ('core', 'z'), pairs)  8.68 us
    ppermute x4, starting transfers between devices, exchange(): return lax.ppermute(value, PAIR, pairs)  4.72 us
    dynamic_slice x4, local copies, waits for them, and re-layouts, block_of(): return lax.dynamic_slice_in_dim(value, index * width, width, axis)  3.32 us
    ppermute x3, starting transfers between devices, layers(): return lax.ppermute(value, ('core', 'z'), pairs)  3.32 us
  transfers between devices with their start and end apart: 20, of which 13 were waited for; matrix products, arithmetic and copies ran while one was open for 9% of the time, Pallas kernels for 1%

profile of v4, /device:TPU:1, one launch (start us, length us, event | category | flops | bytes accessed | tf_op | source)
XLA Modules:
  0.0 96.8 jit_solution(3417022277180161419)
XLA Ops:
  0.0 3.2 %collective-permute-start.6 = (bf16[1,384,6144]{2,1,0:T(8,128)(2,1)}, bf16[1,384,6144]{2,1,0:T(8,128)(2,1)}, u32[]{:S(2)}, u32[]{:S(2)}) collective-permute-start(bf16[1,384,6144]{2,1,0:T(8,128)(2,1)} %param.5), channel_id=1, source_target_pairs={{0,8},{8,0},{1,9},{9,1},{2,10},{10,2},{3,11},{11,3},{4,12},{12,4},... | collective-permute-start | bytes 14155784 | tf_op jit(solution)/shard_map/ppermute | solution.py:40
  4.1 1.4 %copy-done = bf16[64,12288]{1,0:T(8,128)(2,1)S(1)} copy-done((bf16[64,12288]{1,0:T(8,128)(2,1)S(1)}, bf16[64,12288]{1,0:T(8,128)(2,1)}, u32[]{:S(2)}) %copy-start) | copy-done | bytes 1572888
  6.3 2.9 %collective-permute-start.5 = (bf16[64,768]{1,0:T(8,128)(2,1)S(1)}, bf16[64,768]{1,0:T(8,128)(2,1)S(1)}, u32[]{:S(2)}, u32[]{:S(2)}) collective-permute-start(bf16[64,768]{1,0:T(8,128)(2,1)S(1)} %pick.1), channel_id=1, source_target_pairs={{0,6},{1,7},{2,0},{3,1},{4,2},{5,3},{6,4},{7,5},{8,10},{9,11},{10,... | collective-permute-start | bytes 294920 | tf_op jit(solution)/shard_map/ppermute | solution.py:45
  9.2 1.2 %constant_dynamic-slice_fusion.2 = (bf16[176,768]{1,0:T(8,128)(2,1)S(1)}, bf16[176,768]{1,0:T(8,128)(2,1)S(1)}, bf16[176,768]{1,0:T(8,128)(2,1)S(1)}) fusion(bf16[176,6144]{1,0:T(8,128)(2,1)} %param.7, s32[]{:T(128)S(6)} %select_n.99, s32[]{:T(128)S(6)} %select_n.97, s32[]{:T(128)S(6)} %select_n.95), kind=kLoop, calls=%fused_computation.70 | loop fusion | bytes 1622028 | tf_op jit(solution)/shard_map/dynamic_slice | solution.py:98
  10.4 1.8 %collective-permute-done.4 = bf16[64,768]{1,0:T(8,128)(2,1)S(1)} collective-permute-done((bf16[64,768]{1,0:T(8,128)(2,1)S(1)}, bf16[64,768]{1,0:T(8,128)(2,1)S(1)}, u32[]{:S(2)}, u32[]{:S(2)}) %collective-permute-start.4) | collective-permute-done | bytes 98336 | tf_op jit(solution)/shard_map/ppermute | solution.py:45
  12.2 2.9 %collective-permute-done.5 = bf16[64,768]{1,0:T(8,128)(2,1)S(1)} collective-permute-done((bf16[64,768]{1,0:T(8,128)(2,1)S(1)}, bf16[64,768]{1,0:T(8,128)(2,1)S(1)}, u32[]{:S(2)}, u32[]{:S(2)}) %collective-permute-start.5) | collective-permute-done | bytes 98336 | tf_op jit(solution)/shard_map/ppermute | solution.py:45
  15.6 2.8 %collective-permute-start.2 = (bf16[352,768]{1,0:T(8,128)(2,1)S(1)}, bf16[352,768]{1,0:T(8,128)(2,1)S(1)}, u32[]{:S(2)}, u32[]{:S(2)}) collective-permute-start(bf16[352,768]{1,0:T(8,128)(2,1)S(1)} %pad_maximum_fusion.1), channel_id=1, source_target_pairs={{0,48},{8,200},{16,0},{24,216},{32,16},{40,232},{48,32},{56,248},{... | collective-permute-start | bytes 1622024 | tf_op jit(solution)/shard_map/ppermute | solution.py:26
  18.4 4.0 %collective-permute-done.7 = bf16[128,768]{1,0:T(8,128)(2,1)S(1)} collective-permute-done((bf16[128,768]{1,0:T(8,128)(2,1)S(1)}, bf16[128,768]{1,0:T(8,128)(2,1)S(1)}, u32[]{:S(2)}, u32[]{:S(2)}) %collective-permute-start.7) | collective-permute-done | bytes 196640 | tf_op jit(solution)/shard_map/ppermute | solution.py:45
  22.4 1.8 %collective-permute-start.8 = (bf16[256,768]{1,0:T(8,128)(2,1)S(1)}, bf16[256,768]{1,0:T(8,128)(2,1)S(1)}, u32[]{:S(2)}, u32[]{:S(2)}) collective-permute-start(bf16[256,768]{1,0:T(8,128)(2,1)S(1)} %constant_dynamic-update-slice_fusion.3), channel_id=1, source_target_pairs={{0,8},{8,0},{1,9},{9,1},{2,10},{10,2},{3,11},{11,3},{4,12},{12,4},... | collective-permute-start | bytes 1179656 | tf_op jit(solution)/shard_map/ppermute | solution.py:40
  24.3 1.4 %collective-permute-start.3 = (bf16[352,768]{1,0:T(8,128)(2,1)S(1)}, bf16[352,768]{1,0:T(8,128)(2,1)S(1)}, u32[]{:S(2)}, u32[]{:S(2)}) collective-permute-start(bf16[352,768]{1,0:T(8,128)(2,1)S(1)} %pad_maximum_fusion.2), channel_id=1, source_target_pairs={{0,16},{8,72},{16,32},{24,88},{32,48},{40,104},{48,0},{56,120},{64... | collective-permute-start | bytes 1622024 | tf_op jit(solution)/shard_map/ppermute | solution.py:26
  25.7 2.7 %collective-permute-start.1 = (bf16[352,768]{1,0:T(8,128)(2,1)S(1)}, bf16[352,768]{1,0:T(8,128)(2,1)S(1)}, u32[]{:S(2)}, u32[]{:S(2)}) collective-permute-start(bf16[352,768]{1,0:T(8,128)(2,1)S(1)} %pad_maximum_fusion), channel_id=1, source_target_pairs={{0,32},{8,136},{16,48},{24,152},{32,0},{40,168},{48,16},{56,184},{... | collective-permute-start | bytes 1622024 | tf_op jit(solution)/shard_map/ppermute | solution.py:26
  28.4 2.0 %dynamic-slice_bitcast_fusion.4 = (bf16[384,768]{1,0:T(8,128)(2,1)S(1)}, bf16[384,768]{1,0:T(8,128)(2,1)S(1)}, bf16[384,768]{1,0:T(8,128)(2,1)S(1)}, bf16[384,76...) fusion(bf16[1,384,6144]{2,1,0:T(8,128)(2,1)} %collective-permut, ...), kind=kLoop, calls=%fused_computation.34 | loop fusion | bytes 9437200 | tf_op jit(solution)/shard_map/dynamic_slice | solution.py:98
  31.0 0.8 convolution_convert_fusion.2
  33.0 1.4 %collective-permute-start.10 = (bf16[512,768]{1,0:T(8,128)(2,1)S(1)}, bf16[512,768]{1,0:T(8,128)(2,1)S(1)}, u32[]{:S(2)}, u32[]{:S(2)}) collective-permute-start(bf16[512,768]{1,0:T(8,128)(2,1)S(1)} %convolution_convert_fusion.1), channel_id=1, source_target_pairs={{0,16},{8,72},{16,32},{24,88},{32,48},{40,104},{48,0},{56,120},{64... | collective-permute-start | bytes 2359304 | tf_op jit(solution)/shard_map/ppermute | solution.py:26
  35.2 1.6 %collective-permute-start.11 = (bf16[512,768]{1,0:T(8,128)(2,1)S(1)}, bf16[512,768]{1,0:T(8,128)(2,1)S(1)}, u32[]{:S(2)}, u32[]{:S(2)}) collective-permute-start(bf16[512,768]{1,0:T(8,128)(2,1)S(1)} %convolution_convert_fusion), channel_id=1, source_target_pairs={{0,48},{8,200},{16,0},{24,216},{32,16},{40,232},{48,32},{56,248},{... | collective-permute-start | bytes 2359304 | tf_op jit(solution)/shard_map/ppermute | solution.py:26
  36.8 4.3 %collective-permute-done.1 = bf16[352,768]{1,0:T(8,128)(2,1)S(1)} collective-permute-done((bf16[352,768]{1,0:T(8,128)(2,1)S(1)}, bf16[352,768]{1,0:T(8,128)(2,1)S(1)}, u32[]{:S(2)}, u32[]{:S(2)}) %collective-permute-start.1) | collective-permute-done | bytes 540704 | tf_op jit(solution)/shard_map/ppermute | solution.py:26
  41.1 0.8 fusion
  41.9 7.6 %collective-permute-done.9 = bf16[512,768]{1,0:T(8,128)(2,1)S(1)} collective-permute-done((bf16[512,768]{1,0:T(8,128)(2,1)S(1)}, bf16[512,768]{1,0:T(8,128)(2,1)S(1)}, u32[]{:S(2)}, u32[]{:S(2)}) %collective-permute-start.9) | collective-permute-done | bytes 786464 | tf_op jit(solution)/shard_map/ppermute | solution.py:26
  49.6 8.4 %collective-permute-done.10 = bf16[512,768]{1,0:T(8,128)(2,1)S(1)} collective-permute-done((bf16[512,768]{1,0:T(8,128)(2,1)S(1)}, bf16[512,768]{1,0:T(8,128)(2,1)S(1)}, u32[]{:S(2)}, u32[]{:S(2)}) %collective-permute-start.10) | collective-permute-done | bytes 786464 | tf_op jit(solution)/shard_map/ppermute | solution.py:26
  58.3 1.0 %collective-permute-start.12 = (bf16[256,768]{1,0:T(8,128)(2,1)S(1)}, bf16[256,768]{1,0:T(8,128)(2,1)S(1)}, u32[]{:S(2)}, u32[]{:S(2)}) collective-permute-start(bf16[256,768]{1,0:T(8,128)(2,1)S(1)} %get-tuple-element.31), channel_id=1, source_target_pairs={{0,64},{8,24},{16,80},{24,8},{32,96},{40,56},{48,112},{56,40},{64,... | collective-permute-start | bytes 1179656 | tf_op jit(solution)/shard_map/ppermute | solution.py:36
  59.3 1.8 %collective-permute-start.14 = (bf16[256,768]{1,0:T(8,128)(2,1)S(1)}, bf16[256,768]{1,0:T(8,128)(2,1)S(1)}, u32[]{:S(2)}, u32[]{:S(2)}) collective-permute-start(bf16[256,768]{1,0:T(8,128)(2,1)S(1)} %get-tuple-element.32), channel_id=1, source_target_pairs={{0,192},{8,56},{16,208},{24,40},{32,224},{40,24},{48,240},{56,8},{... | collective-permute-start | bytes 1179656 | tf_op jit(solution)/shard_map/ppermute | solution.py:36
  61.2 4.2 %collective-permute-done.12 = bf16[256,768]{1,0:T(8,128)(2,1)S(1)} collective-permute-done((bf16[256,768]{1,0:T(8,128)(2,1)S(1)}, bf16[256,768]{1,0:T(8,128)(2,1)S(1)}, u32[]{:S(2)}, u32[]{:S(2)}) %collective-permute-start.12) | collective-permute-done | bytes 393248 | tf_op jit(solution)/shard_map/ppermute | solution.py:36
  65.4 2.1 %collective-permute-done.14 = bf16[256,768]{1,0:T(8,128)(2,1)S(1)} collective-permute-done((bf16[256,768]{1,0:T(8,128)(2,1)S(1)}, bf16[256,768]{1,0:T(8,128)(2,1)S(1)}, u32[]{:S(2)}, u32[]{:S(2)}) %collective-permute-start.14) | collective-permute-done | bytes 393248 | tf_op jit(solution)/shard_map/ppermute | solution.py:36
  67.7 1.9 %collective-permute-start.13 = (bf16[256,768]{1,0:T(8,128)(2,1)S(1)}, bf16[256,768]{1,0:T(8,128)(2,1)S(1)}, u32[]{:S(2)}, u32[]{:S(2)}) collective-permute-start(bf16[256,768]{1,0:T(8,128)(2,1)S(1)} %get-tuple-element.29), channel_id=1, source_target_pairs={{0,192},{8,56},{16,208},{24,40},{32,224},{40,24},{48,240},{56,8},{... | collective-permute-start | bytes 1179656 | tf_op jit(solution)/shard_map/ppermute | solution.py:36
  69.7 1.0 %dynamic-slice_dynamic-update-slice_fusion.1 = bf16[1408,768]{1,0:T(8,128)(2,1)S(1)} fusion(bf16[1408,768]{1,0:T(8,128)(2,1)S(1)} %constant_dynamic-update-slice_fusion, bf16[176,6144]{1,0:T(8,128)(2,1)} %param.7, s32[]{:T(128)S(6)} %select_n.101), kind=kLoop, calls=%fused_computation.49 | loop fusion | bytes 540676
  70.7 5.2 %collective-permute-done.13 = bf16[256,768]{1,0:T(8,128)(2,1)S(1)} collective-permute-done((bf16[256,768]{1,0:T(8,128)(2,1)S(1)}, bf16[256,768]{1,0:T(8,128)(2,1)S(1)}, u32[]{:S(2)}, u32[]{:S(2)}) %collective-permute-start.13) | collective-permute-done | bytes 393248 | tf_op jit(solution)/shard_map/ppermute | solution.py:36
  76.8 1.3 %fusion.31 = (bf16[1408,512]{1,0:T(8,128)(2,1)S(1)}, f32[1408,512]{1,0:T(8,128)S(1)}) fusion(bf16[1408,768]{1,0:T(8,128)(2,1)S(1)} %dynamic-slice_dynamic-update-slice_fusion, bf16[256,768]{1,0:T(8,128)(2,1)S(1)} %get-tuple-element.28, bf16[256,768]{1,0:T(8,128)(2,1)S(1)} %get-tuple-element.27), kind=kOutput, calls=%fused_computation.85 | convolution fusion | flops 1109590016 | bytes 7274496 | tf_op jit(solution)/shard_map/dot_general | solution.py:148
  79.5 1.9 %collective-permute-start.18 = (bf16[352,512]{1,0:T(8,128)(2,1)S(1)}, bf16[352,512]{1,0:T(8,128)(2,1)S(1)}, u32[]{:S(2)}, u32[]{:S(2)}) collective-permute-start(bf16[352,512]{1,0:T(8,128)(2,1)S(1)} %get-tuple-element.34), channel_id=1, source_target_pairs={{0,48},{8,200},{16,0},{24,216},{32,16},{40,232},{48,32},{56,248},{... | collective-permute-start | bytes 1081352 | tf_op jit(solution)/shard_map/ppermute | solution.py:26
  81.4 5.0 %collective-permute-done.16 = bf16[352,512]{1,0:T(8,128)(2,1)S(1)} collective-permute-done((bf16[352,512]{1,0:T(8,128)(2,1)S(1)}, bf16[352,512]{1,0:T(8,128)(2,1)S(1)}, u32[]{:S(2)}, u32[]{:S(2)}) %collective-permute-start.16) | collective-permute-done | bytes 360480 | tf_op jit(solution)/shard_map/ppermute | solution.py:26
  86.4 3.8 %collective-permute-done.17 = bf16[352,512]{1,0:T(8,128)(2,1)S(1)} collective-permute-done((bf16[352,512]{1,0:T(8,128)(2,1)S(1)}, bf16[352,512]{1,0:T(8,128)(2,1)S(1)}, u32[]{:S(2)}, u32[]{:S(2)}) %collective-permute-start.17) | collective-permute-done | bytes 360480 | tf_op jit(solution)/shard_map/ppermute | solution.py:26
  90.5 4.3 %collective-permute-start.19 = (f32[176,512]{1,0:T(8,128)S(1)}, f32[176,512]{1,0:T(8,128)S(1)}, u32[]{:S(2)}, u32[]{:S(2)}) collective-permute-start(f32[176,512]{1,0:T(8,128)S(1)} %slice.57), channel_id=1, source_target_pairs={{0,8},{8,0},{1,9},{9,1},{2,10},{10,2},{3,11},{11,3},{4,12},{12,4},... | collective-permute-start | bytes 1081352 | tf_op jit(solution)/shard_map/ppermute | solution.py:40
  94.8 1.3 %collective-permute-done.19 = f32[176,512]{1,0:T(8,128)S(1)} collective-permute-done((f32[176,512]{1,0:T(8,128)S(1)}, f32[176,512]{1,0:T(8,128)S(1)}, u32[]{:S(2)}, u32[]{:S(2)}) %collective-permute-start.19) | collective-permute-done | bytes 360480 | tf_op jit(solution)/shard_map/ppermute | solution.py:40
  (56 shorter events, 8.7 us)
Async XLA Ops:
  0.0 15.1 %collective-permute-start.6 = (bf16[1,384,6144]{2,1,0:T(8,128)(2,1)}, bf16[1,384,6144]{2,1,0:T(8,128)(2,1)}, u32[]{:S(2)}, u32[]{:S(2)}) collective-permute-start(bf16[1,384,6144]{2,1,0:T(8,128)(2,1)} %param.5), channel_id=1, source_target_pairs={{0,8},{8,0},{1,9},{9,1},{2,10},{10,2},{3,11},{11,3},{4,12},{12,4},... | collective-permute-start | bytes 14155784 | tf_op jit(solution)/shard_map/ppermute | solution.py:40
  3.2 12.2 %collective-permute-start = (bf16[176,6144]{1,0:T(8,128)(2,1)}, bf16[176,6144]{1,0:T(8,128)(2,1)S(1)}, u32[]{:S(2)}, u32[]{:S(2)}) collective-permute-start(bf16[176,6144]{1,0:T(8,128)(2,1)} %param.7), channel_id=1, source_target_pairs={{0,8},{8,0},{1,9},{9,1},{2,10},{10,2},{3,11},{11,3},{4,12},{12,4},... | collective-permute-start | bytes 6488072 | tf_op jit(solution)/shard_map/ppermute | solution.py:40
  4.1 1.4 %copy-start = (bf16[64,12288]{1,0:T(8,128)(2,1)S(1)}, bf16[64,12288]{1,0:T(8,128)(2,1)}, u32[]{:S(2)}) copy-start(bf16[64,12288]{1,0:T(8,128)(2,1)} %coef_ref.1) | copy-start | bytes 4718596
  6.2 5.9 %collective-permute-start.4 = (bf16[64,768]{1,0:T(8,128)(2,1)S(1)}, bf16[64,768]{1,0:T(8,128)(2,1)S(1)}, u32[]{:S(2)}, u32[]{:S(2)}) collective-permute-start(bf16[64,768]{1,0:T(8,128)(2,1)S(1)} %pick.1), channel_id=1, source_target_pairs={{0,7},{1,0},{2,1},{3,2},{4,3},{5,4},{6,5},{7,6},{8,9},{9,10},{10,1... | collective-permute-start | bytes 294920 | tf_op jit(solution)/shard_map/ppermute | solution.py:45
  6.3 8.7 %collective-permute-start.5 = (bf16[64,768]{1,0:T(8,128)(2,1)S(1)}, bf16[64,768]{1,0:T(8,128)(2,1)S(1)}, u32[]{:S(2)}, u32[]{:S(2)}) collective-permute-start(bf16[64,768]{1,0:T(8,128)(2,1)S(1)} %pick.1), channel_id=1, source_target_pairs={{0,6},{1,7},{2,0},{3,1},{4,2},{5,3},{6,4},{7,5},{8,10},{9,11},{10,... | collective-permute-start | bytes 294920 | tf_op jit(solution)/shard_map/ppermute | solution.py:45
  15.1 7.3 %collective-permute-start.7 = (bf16[128,768]{1,0:T(8,128)(2,1)S(1)}, bf16[128,768]{1,0:T(8,128)(2,1)S(1)}, u32[]{:S(2)}, u32[]{:S(2)}) collective-permute-start(bf16[128,768]{1,0:T(8,128)(2,1)S(1)} %pad_maximum_fusion.4), channel_id=1, source_target_pairs={{0,6},{1,7},{2,0},{3,1},{4,2},{5,3},{6,4},{7,5},{8,10},{9,11},{10,... | collective-permute-start | bytes 589832 | tf_op jit(solution)/shard_map/ppermute | solution.py:45
  15.5 12.9 %copy-start.1 = (bf16[1,384,6144]{2,1,0:T(8,128)(2,1)S(1)}, bf16[1,384,6144]{2,1,0:T(8,128)(2,1)}, u32[]{:S(2)}) copy-start(bf16[1,384,6144]{2,1,0:T(8,128)(2,1)} %param.5) | copy-start | bytes 14155780
  15.6 19.6 %collective-permute-start.2 = (bf16[352,768]{1,0:T(8,128)(2,1)S(1)}, bf16[352,768]{1,0:T(8,128)(2,1)S(1)}, u32[]{:S(2)}, u32[]{:S(2)}) collective-permute-start(bf16[352,768]{1,0:T(8,128)(2,1)S(1)} %pad_maximum_fusion.1), channel_id=1, source_target_pairs={{0,48},{8,200},{16,0},{24,216},{32,16},{40,232},{48,32},{56,248},{... | collective-permute-start | bytes 1622024 | tf_op jit(solution)/shard_map/ppermute | solution.py:26
  22.4 8.0 %collective-permute-start.8 = (bf16[256,768]{1,0:T(8,128)(2,1)S(1)}, bf16[256,768]{1,0:T(8,128)(2,1)S(1)}, u32[]{:S(2)}, u32[]{:S(2)}) collective-permute-start(bf16[256,768]{1,0:T(8,128)(2,1)S(1)} %constant_dynamic-update-slice_fusion.3), channel_id=1, source_target_pairs={{0,8},{8,0},{1,9},{9,1},{2,10},{10,2},{3,11},{11,3},{4,12},{12,4},... | collective-permute-start | bytes 1179656 | tf_op jit(solution)/shard_map/ppermute | solution.py:40
  24.3 12.6 %collective-permute-start.3 = (bf16[352,768]{1,0:T(8,128)(2,1)S(1)}, bf16[352,768]{1,0:T(8,128)(2,1)S(1)}, u32[]{:S(2)}, u32[]{:S(2)}) collective-permute-start(bf16[352,768]{1,0:T(8,128)(2,1)S(1)} %pad_maximum_fusion.2), channel_id=1, source_target_pairs={{0,16},{8,72},{16,32},{24,88},{32,48},{40,104},{48,0},{56,120},{64... | collective-permute-start | bytes 1622024 | tf_op jit(solution)/shard_map/ppermute | solution.py:26
  25.7 15.5 %collective-permute-start.1 = (bf16[352,768]{1,0:T(8,128)(2,1)S(1)}, bf16[352,768]{1,0:T(8,128)(2,1)S(1)}, u32[]{:S(2)}, u32[]{:S(2)}) collective-permute-start(bf16[352,768]{1,0:T(8,128)(2,1)S(1)} %pad_maximum_fusion), channel_id=1, source_target_pairs={{0,32},{8,136},{16,48},{24,152},{32,0},{40,168},{48,16},{56,184},{... | collective-permute-start | bytes 1622024 | tf_op jit(solution)/shard_map/ppermute | solution.py:26
  31.8 17.8 %collective-permute-start.9 = (bf16[512,768]{1,0:T(8,128)(2,1)S(1)}, bf16[512,768]{1,0:T(8,128)(2,1)S(1)}, u32[]{:S(2)}, u32[]{:S(2)}) collective-permute-start(bf16[512,768]{1,0:T(8,128)(2,1)S(1)} %convolution_convert_fusion.2), channel_id=1, source_target_pairs={{0,32},{8,136},{16,48},{24,152},{32,0},{40,168},{48,16},{56,184},{... | collective-permute-start | bytes 2359304 | tf_op jit(solution)/shard_map/ppermute | solution.py:26
  33.0 24.9 %collective-permute-start.10 = (bf16[512,768]{1,0:T(8,128)(2,1)S(1)}, bf16[512,768]{1,0:T(8,128)(2,1)S(1)}, u32[]{:S(2)}, u32[]{:S(2)}) collective-permute-start(bf16[512,768]{1,0:T(8,128)(2,1)S(1)} %convolution_convert_fusion.1), channel_id=1, source_target_pairs={{0,16},{8,72},{16,32},{24,88},{32,48},{40,104},{48,0},{56,120},{64... | collective-permute-start | bytes 2359304 | tf_op jit(solution)/shard_map/ppermute | solution.py:26
  35.2 22.8 %collective-permute-start.11 = (bf16[512,768]{1,0:T(8,128)(2,1)S(1)}, bf16[512,768]{1,0:T(8,128)(2,1)S(1)}, u32[]{:S(2)}, u32[]{:S(2)}) collective-permute-start(bf16[512,768]{1,0:T(8,128)(2,1)S(1)} %convolution_convert_fusion), channel_id=1, source_target_pairs={{0,48},{8,200},{16,0},{24,216},{32,16},{40,232},{48,32},{56,248},{... | collective-permute-start | bytes 2359304 | tf_op jit(solution)/shard_map/ppermute | solution.py:26
  58.3 7.0 %collective-permute-start.12 = (bf16[256,768]{1,0:T(8,128)(2,1)S(1)}, bf16[256,768]{1,0:T(8,128)(2,1)S(1)}, u32[]{:S(2)}, u32[]{:S(2)}) collective-permute-start(bf16[256,768]{1,0:T(8,128)(2,1)S(1)} %get-tuple-element.31), channel_id=1, source_target_pairs={{0,64},{8,24},{16,80},{24,8},{32,96},{40,56},{48,112},{56,40},{64,... | collective-permute-start | bytes 1179656 | tf_op jit(solution)/shard_map/ppermute | solution.py:36
  59.3 8.1 %collective-permute-start.14 = (bf16[256,768]{1,0:T(8,128)(2,1)S(1)}, bf16[256,768]{1,0:T(8,128)(2,1)S(1)}, u32[]{:S(2)}, u32[]{:S(2)}) collective-permute-start(bf16[256,768]{1,0:T(8,128)(2,1)S(1)} %get-tuple-element.32), channel_id=1, source_target_pairs={{0,192},{8,56},{16,208},{24,40},{32,224},{40,24},{48,240},{56,8},{... | collective-permute-start | bytes 1179656 | tf_op jit(solution)/shard_map/ppermute | solution.py:36
  67.7 8.2 %collective-permute-start.13 = (bf16[256,768]{1,0:T(8,128)(2,1)S(1)}, bf16[256,768]{1,0:T(8,128)(2,1)S(1)}, u32[]{:S(2)}, u32[]{:S(2)}) collective-permute-start(bf16[256,768]{1,0:T(8,128)(2,1)S(1)} %get-tuple-element.29), channel_id=1, source_target_pairs={{0,192},{8,56},{16,208},{24,40},{32,224},{40,24},{48,240},{56,8},{... | collective-permute-start | bytes 1179656 | tf_op jit(solution)/shard_map/ppermute | solution.py:36
  69.6 6.9 %collective-permute-start.15 = (bf16[256,768]{1,0:T(8,128)(2,1)S(1)}, bf16[256,768]{1,0:T(8,128)(2,1)S(1)}, u32[]{:S(2)}, u32[]{:S(2)}) collective-permute-start(bf16[256,768]{1,0:T(8,128)(2,1)S(1)} %get-tuple-element.30), channel_id=1, source_target_pairs={{0,64},{8,24},{16,80},{24,8},{32,96},{40,56},{48,112},{56,40},{64,... | collective-permute-start | bytes 1179656 | tf_op jit(solution)/shard_map/ppermute | solution.py:36
  78.2 8.2 %collective-permute-start.16 = (bf16[352,512]{1,0:T(8,128)(2,1)S(1)}, bf16[352,512]{1,0:T(8,128)(2,1)S(1)}, u32[]{:S(2)}, u32[]{:S(2)}) collective-permute-start(bf16[352,512]{1,0:T(8,128)(2,1)S(1)} %get-tuple-element.33), channel_id=1, source_target_pairs={{0,32},{8,136},{16,48},{24,152},{32,0},{40,168},{48,16},{56,184},{... | collective-permute-start | bytes 1081352 | tf_op jit(solution)/shard_map/ppermute | solution.py:26
  78.8 11.5 %collective-permute-start.17 = (bf16[352,512]{1,0:T(8,128)(2,1)S(1)}, bf16[352,512]{1,0:T(8,128)(2,1)S(1)}, u32[]{:S(2)}, u32[]{:S(2)}) collective-permute-start(bf16[352,512]{1,0:T(8,128)(2,1)S(1)} %get-tuple-element.35), channel_id=1, source_target_pairs={{0,16},{8,72},{16,32},{24,88},{32,48},{40,104},{48,0},{56,120},{64... | collective-permute-start | bytes 1081352 | tf_op jit(solution)/shard_map/ppermute | solution.py:26
  79.5 10.7 %collective-permute-start.18 = (bf16[352,512]{1,0:T(8,128)(2,1)S(1)}, bf16[352,512]{1,0:T(8,128)(2,1)S(1)}, u32[]{:S(2)}, u32[]{:S(2)}) collective-permute-start(bf16[352,512]{1,0:T(8,128)(2,1)S(1)} %get-tuple-element.34), channel_id=1, source_target_pairs={{0,48},{8,200},{16,0},{24,216},{32,16},{40,232},{48,32},{56,248},{... | collective-permute-start | bytes 1081352 | tf_op jit(solution)/shard_map/ppermute | solution.py:26
  90.5 5.6 %collective-permute-start.19 = (f32[176,512]{1,0:T(8,128)S(1)}, f32[176,512]{1,0:T(8,128)S(1)}, u32[]{:S(2)}, u32[]{:S(2)}) collective-permute-start(f32[176,512]{1,0:T(8,128)S(1)} %slice.57), channel_id=1, source_target_pairs={{0,8},{8,0},{1,9},{9,1},{2,10},{10,2},{3,11},{11,3},{4,12},{12,4},... | collective-permute-start | bytes 1081352 | tf_op jit(solution)/shard_map/ppermute | solution.py:40
